TPU v7x, 32 devices: a whole 2x2x4 slice. The times are simulated.
32 devices in a mesh: img: 8 (over z, y), seq: 4 (over x, core).
Axes of the slice: x: 2, y: 2, z: 4, core: 2. Of those that a mesh axis runs over, the one named last changes fastest.
Arguments:
- tokens: float32 [8, 4096, 384], P('img', 'seq'), may hold values from -6 to 6
- valid_mask: int32 [8, 4096], P('img', 'seq'), may hold values from 0 to 1, as said below
- timesteps: int32 [8], P('img'), may hold values from 0 to 999
- class_ids: int32 [8], P('img'), may hold values from 0 to 999
- time_first: float32 [256, 384], replicated, may hold values from -0.375 to 0.375
- time_second: float32 [384, 384], replicated, may hold values from -0.3125 to 0.3125
- class_table: float32 [1000, 384], replicated, may hold values from -6 to 6
- ada_weight: float32 [384, 2304], replicated, may hold values from -0.3125 to 0.3125
- ada_bias: float32 [2304], replicated, may hold values from -3 to 3
- conv_taps: float32 [9, 384], replicated, may hold values from -2 to 2
- query_proj: float32 [384, 384], replicated, may hold values from -0.3125 to 0.3125
- key_proj: float32 [384, 384], replicated, may hold values from -0.3125 to 0.3125
- value_proj: float32 [384, 384], replicated, may hold values from -0.3125 to 0.3125
- decay_down: float32 [384, 16], replicated, may hold values from -0.3125 to 0.3125
- decay_up: float32 [16, 384], replicated, may hold values from -1.5 to 1.5
- decay_bias: float32 [384], replicated, may hold values from 0.5 to 6
- gate_proj: float32 [384, 384], replicated, may hold values from -0.3125 to 0.3125
- out_proj: float32 [384, 384], replicated, may hold values from -0.625 to 0.625
- mlp_up: float32 [384, 1536], replicated, may hold values from -0.3125 to 0.3125
- mlp_down: float32 [1536, 384], replicated, may hold values from -0.3125 to 0.3125
- cotangent: float32 [8, 4096, 384], P('img', 'seq'), may hold values from -6 to 6
Outputs:
- block_out: float32 [8, 4096, 384], P('img', 'seq')
- tokens_grad: float32 [8, 4096, 384], P('img', 'seq')
- time_first_grad: float32 [256, 384], replicated
- time_second_grad: float32 [384, 384], replicated
- class_table_grad: float32 [1000, 384], replicated
- ada_weight_grad: float32 [384, 2304], replicated
- ada_bias_grad: float32 [2304], replicated
- conv_taps_grad: float32 [9, 384], replicated
- query_proj_grad: float32 [384, 384], replicated
- key_proj_grad: float32 [384, 384], replicated
- value_proj_grad: float32 [384, 384], replicated
- decay_down_grad: float32 [384, 16], replicated
- decay_up_grad: float32 [16, 384], replicated
- decay_bias_grad: float32 [384], replicated
- gate_proj_grad: float32 [384, 384], replicated
- out_proj_grad: float32 [384, 384], replicated
- mlp_up_grad: float32 [384, 1536], replicated
- mlp_down_grad: float32 [1536, 384], replicated
Inputs may be any that keep to these rules, and one draw needn't show every extreme that they name: `valid_mask`: in each image the real patches are the first L of its 4096 patches, with 1024 <= L < 4096.
All inputs are finite; a program needn't handle non-finite values.
Results may differ from a plain program's by a relative error of at most 0.0003.
Values sent between devices are 32-bit elements; how exact they have to be, the bound alone decides.
No kernel may reach another device: no remote copies, remote signals or barrier semaphores. Data moves between devices by JAX's collectives and lax.ppermute only.
A program may use at most 320 MiB of HBM per device.

v0:
```python
import math

import jax
import jax.numpy as jnp
from jax import lax
from jax.sharding import PartitionSpec as P

HEADS = 6
HEAD_DIM = 64
CLASSES = 1000
FREQ = 256
GRID = 64
STRETCH = 64


HIGH = lax.Precision.HIGHEST


def extended(shard, sides, width):
    for axis, dim in sides:
        size, length = (lax.axis_size(axis), shard.shape[dim])
        up = [(i, (i + 1) % size) for i in range(size - 1)]
        down = [(j, i) for i, j in up]
        last = lax.slice_in_dim(shard, length - width, length, axis=dim)
        leading = lax.slice_in_dim(shard, 0, width, axis=dim)
        before = lax.ppermute(last, axis, up)
        after = lax.ppermute(leading, axis, down)
        shard = jnp.concatenate([before, shard, after], axis=dim)
    return shard


def carried_in(value, axis, join, neutral, backward):
    count, mine = (lax.axis_size(axis), lax.axis_index(axis))
    pieces = jax.tree.map(lambda part: lax.all_gather(part, axis), value)
    if backward:
        pieces = jax.tree.map(lambda part: part[::-1], pieces)
        mine = count - 1 - mine
    total = jax.tree.map(
        lambda part, zero: jnp.full_like(part, 0) + jnp.asarray(zero, part.dtype), value, neutral
    )

    def lap(position, total):
        longer = join(total, jax.tree.map(lambda part: part[position], pieces))
        return jax.tree.map(lambda new, old: jnp.where(position < mine, new, old), longer, total)

    return lax.fori_loop(0, count - 1, lap, total)


def product(left, right):
    return jnp.dot(left, right, precision=HIGH, preferred_element_type=jnp.float32)


def time_features(timesteps):
    half = FREQ // 2
    freqs = jnp.exp(-math.log(10000.0) * jnp.arange(half, dtype=jnp.float32) / half)
    angles = timesteps.astype(jnp.float32)[:, None] * freqs[None, :]
    return jnp.concatenate([jnp.cos(angles), jnp.sin(angles)], axis=1)


def condition(timesteps, class_ids, time_first, time_second, class_table, ada_weight, ada_bias):
    embed = product(jax.nn.silu(product(time_features(timesteps), time_first)), time_second)
    onehot = (class_ids[:, None] == jnp.arange(CLASSES, dtype=jnp.int32)[None, :]).astype(
        jnp.float32
    )
    embed = embed + product(onehot, class_table)
    return product(jax.nn.silu(embed), ada_weight) + ada_bias


def layer_norm(values):
    center = values - jnp.mean(values, axis=-1, keepdims=True)
    return center * lax.rsqrt(jnp.mean(center * center, axis=-1, keepdims=True) + 1e-06)


def pair_mix(query, keys, values, cumul):
    diff = cumul[..., :, None, :, :] - cumul[..., None, :, :, :]
    size = cumul.shape[-3]
    causal = (jnp.arange(size)[:, None] >= jnp.arange(size)[None, :])[:, :, None, None]
    weight = jnp.where(causal, jnp.exp(jnp.where(causal, diff, 0.0)), 0.0)
    scores = jnp.sum(query[..., :, None, :, :] * keys[..., None, :, :, :] * weight, axis=-1)
    return jnp.einsum("...tsh,...she->...the", scores, values, precision=HIGH)


def chain_join(earlier, later):
    return (later[0] * earlier[0], later[0][..., None] * earlier[1] + later[1])


def front(tokens, modul):
    pieces = jnp.split(modul, 6, axis=1)
    return layer_norm(tokens) * (1.0 + pieces[1][:, None]) + pieces[0][:, None]


def mixer_front(
    padded, keep, conv_taps, query_proj, key_proj, value_proj, decay_down, decay_up, decay_bias
):
    count, span, width = padded.shape
    length = span - 2 * GRID
    lines = length // GRID
    grid = jnp.pad(padded.reshape(count, lines + 2, GRID, width), ((0, 0), (0, 0), (1, 1), (0, 0)))
    mixed = jnp.zeros((count, lines, GRID, width), jnp.float32)
    for row in range(3):
        for col in range(3):
            mixed = mixed + conv_taps[row * 3 + col] * grid[:, row : row + lines, col : col + GRID]
    hidden = jax.nn.silu(mixed.reshape(count, length, width))
    query = product(hidden, query_proj) * HEAD_DIM ** (-0.5)
    keys = product(hidden, key_proj) * keep
    values = product(hidden, value_proj) * keep
    gates = (
        jax.nn.log_sigmoid(product(product(hidden, decay_down), decay_up) + decay_bias)
        / 16.0
        * keep
    )
    blocks = length // STRETCH

    def shaped(array):
        return array.reshape(count, blocks, STRETCH, HEADS, HEAD_DIM)

    query, keys, values, gates = (shaped(query), shaped(keys), shaped(values), shaped(gates))
    cumul = jnp.cumsum(gates, axis=2)
    group = math.gcd(count, max(1, 512 // length))

    def grouped(array):
        return array.reshape((count // group, group) + array.shape[1:])

    inner = lax.map(
        jax.checkpoint(lambda items: pair_mix(*items)),
        (grouped(query), grouped(keys), grouped(values), grouped(cumul)),
    )
    inner = inner.reshape(query.shape)
    decayed_query = query * jnp.exp(cumul)
    final = cumul[:, :, -1]
    carried = jnp.einsum(
        "ncshd,ncshe->nchde", keys * jnp.exp(final[:, :, None] - cumul), values, precision=HIGH
    )
    fades = jnp.exp(final)

    def advance(carry, items):
        total_fade, total_state = carry
        fade, state = items
        return (
            (fade * total_fade, fade[..., None] * total_state + state),
            (total_fade, total_state),
        )

    start = (jnp.ones_like(fades[:, 0]), jnp.zeros_like(carried[:, 0]))
    (dev_fade, dev_state), (pre_fade, pre_state) = lax.scan(
        advance, start, (jnp.moveaxis(fades, 1, 0), jnp.moveaxis(carried, 1, 0))
    )
    return (inner, decayed_query, pre_state, pre_fade, dev_fade, dev_state)


def tail(
    inner,
    decayed_query,
    pre_state,
    pre_fade,
    state_in,
    tokens,
    normed,
    modul,
    gate_proj,
    out_proj,
    mlp_up,
    mlp_down,
):
    count, length, width = tokens.shape
    shift_a, scale_a, gate_a, shift_b, scale_b, gate_b = jnp.split(modul, 6, axis=1)
    enter = pre_state + pre_fade[..., None] * state_in[None]
    outer = jnp.einsum("ncthd,cnhde->ncthe", decayed_query, enter, precision=HIGH)
    attended = (inner + outer).reshape(count, length, HEADS, HEAD_DIM)
    attended = attended * lax.rsqrt(jnp.mean(attended * attended, axis=-1, keepdims=True) + 1e-05)
    branch = product(
        attended.reshape(count, length, width) * jax.nn.silu(product(normed, gate_proj)), out_proj
    )
    middle = tokens + gate_a[:, None] * branch
    second = layer_norm(middle) * (1.0 + scale_b[:, None]) + shift_b[:, None]
    return middle + gate_b[:, None] * product(jax.nn.gelu(product(second, mlp_up)), mlp_down)


def body(
    tokens,
    valid_mask,
    timesteps,
    class_ids,
    time_first,
    time_second,
    class_table,
    ada_weight,
    ada_bias,
    conv_taps,
    query_proj,
    key_proj,
    value_proj,
    decay_down,
    decay_up,
    decay_bias,
    gate_proj,
    out_proj,
    mlp_up,
    mlp_down,
    cotangent,
):
    length = tokens.shape[1]

    def embed(first, second, table, weight, bias):
        return condition(timesteps, class_ids, first, second, table, weight, bias)

    modul, pull_embed = jax.vjp(embed, time_first, time_second, class_table, ada_weight, ada_bias)
    normed, pull_front = jax.vjp(front, tokens, modul)
    padded = extended(normed, (("seq", 1),), GRID)
    keep = valid_mask.astype(jnp.float32)[..., None]

    def mixer(pad_in, taps, q_weight, k_weight, v_weight, down_weight, up_weight, bias_in):
        return mixer_front(
            pad_in, keep, taps, q_weight, k_weight, v_weight, down_weight, up_weight, bias_in
        )

    parts, pull_mixer = jax.vjp(
        mixer, padded, conv_taps, query_proj, key_proj, value_proj, decay_down, decay_up, decay_bias
    )
    inner, decayed_query, pre_state, pre_fade, dev_fade, dev_state = parts
    state_in = carried_in(
        (dev_fade, dev_state),
        "seq",
        chain_join,
        (jnp.ones_like(dev_fade), jnp.zeros_like(dev_state)),
        False,
    )[1]
    block_out, pull_tail = jax.vjp(
        tail,
        inner,
        decayed_query,
        pre_state,
        pre_fade,
        state_in,
        tokens,
        normed,
        modul,
        gate_proj,
        out_proj,
        mlp_up,
        mlp_down,
    )
    (
        d_inner,
        d_query,
        d_pre_state,
        d_pre_fade,
        d_state,
        dx_tail,
        dn_tail,
        dmod_tail,
        g_gate,
        g_out,
        g_up,
        g_down,
    ) = pull_tail(cotangent)
    d_outgoing = carried_in(
        (dev_fade, d_state),
        "seq",
        chain_join,
        (jnp.ones_like(dev_fade), jnp.zeros_like(d_state)),
        True,
    )[1]
    d_dev_fade = jnp.sum(d_outgoing * state_in, axis=-1)
    pulled = pull_mixer((d_inner, d_query, d_pre_state, d_pre_fade, d_dev_fade, d_outgoing))
    d_pad = pulled[0]
    rims = jnp.concatenate([d_pad[:, :GRID], d_pad[:, -GRID:]], axis=1)
    beside_all = extended(rims, (("seq", 1),), GRID)
    d_normed = d_pad[:, GRID:-GRID] + dn_tail
    d_normed = d_normed + jnp.pad(beside_all[:, :GRID], ((0, 0), (0, length - GRID), (0, 0)))
    d_normed = d_normed + jnp.pad(beside_all[:, -GRID:], ((0, 0), (length - GRID, 0), (0, 0)))
    dx_front, dmod_front = pull_front(d_normed)
    tokens_grad = dx_tail + dx_front
    embed_grads = pull_embed(dmod_tail + dmod_front)
    first_grads = tuple(embed_grads) + tuple(pulled[1:])
    summed = lax.psum(first_grads + (g_gate, g_out, g_up, g_down), ("img", "seq"))
    return (
        block_out,
        tokens_grad,
        summed[0],
        summed[1],
        summed[2],
        summed[3],
        summed[4],
        summed[5],
        summed[6],
        summed[7],
        summed[8],
        summed[9],
        summed[10],
        summed[11],
        summed[12],
        summed[13],
        summed[14],
        summed[15],
    )


def solution(mesh):
    placed = (
        P("img", "seq", None),
        P("img", "seq"),
        P("img"),
        P("img"),
        P(),
        P(),
        P(),
        P(),
        P(),
        P(),
        P(),
        P(),
        P(),
        P(),
        P(),
        P(),
        P(),
        P(),
        P(),
        P(),
        P("img", "seq", None),
    )
    return jax.shard_map(
        body,
        mesh=mesh,
        in_specs=placed,
        out_specs=(
            P("img", "seq", None),
            P("img", "seq", None),
            P(),
            P(),
            P(),
            P(),
            P(),
            P(),
            P(),
            P(),
            P(),
            P(),
            P(),
            P(),
            P(),
            P(),
            P(),
            P(),
        ),
        check_vma=False,
    )
```

profile of v0, /device:TPU:0, one launch (start us, length us, event | category | flops | bytes accessed | tf_op | source)
XLA Modules:
  0.0 1686.7 jit_solution(18301640404507162143)
XLA Ops:
  54.7 8.6 divide_multiply_fusion
  168.6 105.6 %while.81 = (s32[]{:T(128)}, f32[1,6,64]{2,1,0:T(8,128)S(1)}, f32[1,6,64,64]{3,2,1,0:T(8,128)}, f32[16,1,6,64]{3,2,1,0:T(8,128)}, f32[16,1,6,64,64]{4,3,2,1,0:T(...) while((s32[]{:T(128)}, f32[1,6,64]{2,1,0:T(8,128)S(1)}, ...), condition=%wide.region_5.6_spmd.clone, body=%wide.region_4.5_spmd.clone.sunk | while | flops 99459 | bytes 711314 | solution.py:145
  281.3 11.8 all-gather.1
  305.8 8.5 fusion.38
  314.4 83.2 %multiply_reduce_fusion.2 = f32[16,64,64,6]{2,3,1,0:T(8,128)} fusion(f32[16,64,6,64]{3,1,2,0:T(8,128)} %copy.357, f32[16,64,6,64]{3,2,1,0:T(8,128)} %copy.356, f32[16,64,6,64]{3,1,2,0:T(8,128)} %copy.353, f32[16,64,6,64]{3,2,1,0:T(8,128)} %copy.351, pred[64,64]{1,0:T(8,128)(4,1)S(1)} %copy-done.111), kind=kLoop, calls=%fused_computation.36 | loop fusion | flops 150601728 | bytes 7868416 | tf_op jit(solution)/shard_map/jvp()/while/body/eval_jaxpr/reduce_sum | solution.py:79
  397.5 8.8 multiply_reduce_fusion.6
  432.2 10.4 fusion.91
  442.7 13.2 fusion.77
  455.9 13.3 fusion.53
  469.2 13.6 fusion.19
  482.9 11.6 fusion.173
  494.5 9.7 fusion.89
  555.5 7.8 multiply_reduce_fusion.3
  565.0 10.0 all-gather.2
  588.4 154.1 %while.80 = (s32[]{:T(128)}, f32[1,6,64]{2,1,0:T(8,128)S(1)}, f32[1,6,64,64]{3,2,1,0:T(8,128)}, f32[16,1,6,64]{3,0,2,1:T(8,128)}, f32[16,1,6,64,64]{4,3,2,1,0:T(...) while((s32[]{:T(128)}, f32[1,6,64]{2,1,0:T(8,128)S(1)}, ...), condition=%wide.region_21.22_spmd, body=%wide.region_19.21_spmd.sunk | while | flops 99459 | bytes 1202857 | solution.py:145
  742.4 9.9 fusion.35
  752.3 7.8 fusion.33
  789.1 7.8 fusion.63
  801.1 253.6 %fusion.13 = (f32[16,64,6,64]{3,1,2,0:T(8,128)}, f32[16,64,6,64]{3,2,1,0:T(8,128)}, f32[16,64,6,64]{3,1,2,0:T(8,128)}, f32[16,64,64,6]{2,3,1,0:T(8,128)}, f32[16,64,6,64]{3,2,1,0:T(8,128)}) fusion(f32[16,64,6,64]{3,1,2,0:T(8,128)} %copy.410, f32[16,64,6,64]{3,2,1,0:T(8,128)S(1)} %copy-done.36, f32[16,64,64,6]{2,3,1,0:T(8,128)} %copy.408, ...), kind=kLoop, calls=%fused_computation.35 | loop fusion | flops 425852928 | bytes 15732736 | tf_op jit(solution)/shard_map/transpose(jvp())/while/body/eval_jaxpr/checkpoint/reduce_sum | solution.py:75
  1065.3 12.9 fusion.133
  1078.2 21.7 %broadcast_multiply_fusion.2 = (f32[1,16,64,6,64]{4,1,3,2,0:T(8,128)}, f32[1,16,64,6,64]{4,1,3,2,0:T(8,128)}, f32[1,16,64,6,64]{4,1,3,2,0:T(8,128)}, f32[1,16,64,6,64]{4,1,3,2,0:T(8,128)}, f32[1,16,64,6,64]{4,1,3,2,0:T(8,128)}) fusion(f32[16,64]{0,1:T(8,128)S(1)} %copy-done.69, f32[16,64,6,64]{3,1,2,0:T(8,128)} %get-tuple-element.880, ...), kind=kLoop, calls=%fused_computation.165 | loop fusion | flops 6291456 | bytes 23646208 | tf_op jit(solution)/shard_map/transpose(jvp())/mul | solution.py:105
  1128.5 7.9 fusion.175
  1273.9 116.6 %all-reduce.27.cloned.1.call-done = (f32[2304]{0:T(1024)}, f32[9,384]{1,0:T(8,128)}, f32[384,16]{0,1:T(8,128)}, f32[16,384]{1,0:T(8,128)}, f32[384]{0:T(512)}) async-done(((f32[2304]{0:T(1024)}, f32[9,384]{1,0:T(8,128)}, f32[384,16]{0,1:T(8,128)}, f32[16,384]{1,0:T(8,128)}, f32[384]{0:T(512)}), (f32[2304]{0:T(1024)}, f32[9,384]{1,0:T(8,128)}, f32[384,16]{0,1:T(8,128)}, f32[16,384]{1,0:T(8,128)}, ...) | async-done | bytes 73744 | tf_op jit(solution)/shard_map/psum | solution.py:276
  1390.5 269.6 %all-reduce.29.cloned.1.call-done = (f32[256,384]{1,0:T(8,128)}, f32[384,384]{1,0:T(8,128)}, f32[1000,384]{1,0:T(8,128)}, f32[384,2304]{1,0:T(8,128)}, f32[384,3...) async-done(((f32[256,384]{1,0:T(8,128)}, ...) | async-done | bytes 13725712 | tf_op jit(solution)/shard_map/psum | solution.py:276
  (717 shorter events, 765.7 us)
Async XLA Ops:
  7.2 14.7 copy-start
  27.3 21.4 %collective-permute-start.1 = (f32[1,64,384]{1,2,0:T(8,128)}, f32[1,64,384]{1,2,0:T(8,128)}, u32[]{:S(2)}, u32[]{:S(2)}) collective-permute-start(f32[1,64,384]{1,2,0:T(8,128)} %get-tuple-element.1026), channel_id=1, source_target_pairs={{1,0},{2,1},{3,2},{5,4},{6,5},{7,6},{9,8},{10,9},{11,10},{13,12},{... | collective-permute-start | bytes 294920 | tf_op jit(solution)/shard_map/ppermute | solution.py:27
  28.6 20.1 %collective-permute-start = (f32[1,64,384]{1,2,0:T(8,128)}, f32[1,64,384]{1,2,0:T(8,128)}, u32[]{:S(2)}, u32[]{:S(2)}) collective-permute-start(f32[1,64,384]{1,2,0:T(8,128)} %get-tuple-element.1027), channel_id=1, source_target_pairs={{0,1},{1,2},{2,3},{4,5},{5,6},{6,7},{8,9},{9,10},{10,11},{12,13},{... | collective-permute-start | bytes 294920 | tf_op jit(solution)/shard_map/ppermute | solution.py:26
  32.3 79.3 %copy-start.64 = (f32[1,1024]{1,0:T(1,128)}, f32[1,1024]{1,0:T(1,128)S(1)}, u32[]{:S(2)}) copy-start(f32[1,1024]{1,0:T(1,128)S(1)} %convert_element_type.14) | copy-start | bytes 12292
  37.2 17.5 %copy-start.95 = (f32[384]{0:T(512)}, f32[384]{0:T(512)S(1)}, u32[]{:S(2)}) copy-start(f32[384]{0:T(512)S(1)} %get-tuple-element.900) | copy-start | bytes 4612
  280.7 12.4 copy-start.68
  314.4 83.2 %copy-start.8 = (f32[16,64,6,64]{3,1,2,0:T(8,128)S(1)}, f32[16,64,6,64]{3,1,2,0:T(8,128)}, u32[]{:S(2)}) copy-start(f32[16,64,6,64]{3,1,2,0:T(8,128)} %copy.363) | copy-start | bytes 4718596
  431.6 62.9 %copy-start.9 = (f32[1,1024,384]{1,2,0:T(8,128)}, f32[1,1024,384]{1,2,0:T(8,128)S(1)}, u32[]{:S(2)}) copy-start(f32[1,1024,384]{1,2,0:T(8,128)S(1)} %get-tuple-element.1000) | copy-start | bytes 4718596
  432.2 10.4 copy-start.129
  442.7 13.2 copy-start.114
  801.1 253.6 %copy-start.5 = (f32[1,16,64,6,64]{2,4,3,1,0:T(8,128)S(1)}, f32[1,16,64,6,64]{2,4,3,1,0:T(8,128)}, u32[]{:S(2)}) copy-start(f32[1,16,64,6,64]{2,4,3,1,0:T(8,128)} %copy-done.4) | copy-start | bytes 4718596
  1065.3 12.9 copy-start.3
  1065.3 12.9 copy-start.66
  1065.3 12.9 copy-start.49
  1065.3 12.9 copy-start.69
  1212.1 10.6 copy-start.120
  1224.9 12.3 copy-start.109
  1224.9 13.6 copy-start.110
  1224.9 17.6 %copy-start.71 = (f32[1024]{0:T(1024)S(1)}, f32[1024]{0:T(1024)}, u32[]{:S(2)}) copy-start(f32[1024]{0:T(1024)} %copy-done.70) | copy-start | bytes 12292
  1224.9 17.6 %copy-start.80 = (f32[384]{0:T(512)S(1)}, f32[384]{0:T(512)}, u32[]{:S(2)}) copy-start(f32[384]{0:T(512)} %copy-done.79) | copy-start | bytes 4612
  1231.4 11.2 collective-permute-start.3
  1232.7 9.9 collective-permute-start.2
  1257.7 132.9 %all-reduce.27.cloned.1.call-start = ((), (), s32[]{:S(2)}) async-start(), calls=%async_computation | async-start | bytes 176128 | tf_op jit(solution)/shard_map/psum | solution.py:276
  1262.1 398.0 %all-reduce.29.cloned.1.call-start = ((), (), s32[]{:S(2)}) async-start(), calls=%async_computation.1 | async-start | bytes 27451392 | tf_op jit(solution)/shard_map/psum | solution.py:276
  (116 other events, 486.8 us)
Sparse Core Ops, SparseCore 0:
  1266.1 124.4 all-reduce.26
  1398.7 261.4 all-reduce.28
where the time goes:
time: 1700 us; the launch traced here: 1690 us
  other arithmetic  566 us (33%)
  local copies, waits for them, and re-layouts  415 us (24%)
  waiting for transfers between devices  386 us (23%)
  matrix products  264 us (16%)
  blocking collectives  28.5 us (2%)
  between operations  17.3 us (1%)
    psum x2, waiting for transfers between devices, body(): lax.psum(first_grads + (g_gate, g_out, g_up, g_down), ('img', 'seq'))  386 us
    reduce_sum x1, other arithmetic, pair_mix(): diff = cumul[..., :, None, :, :] - cumul[..., None, :, :, :]  254 us
    dot_general x33, matrix products, product(): jnp.dot(left, right, precision=HIGH, preferred_element_type=jnp.float32)  192 us
    reduce_sum x1, other arithmetic, pair_mix(): jnp.sum(query[..., :, None, :, :] * keys[..., None, :, :, :] * weight, ax...  83.2 us
    dynamic_update_slice x64, local copies, waits for them, and re-layouts, mixer_front(): lax.scan(advance, start, (jnp.moveaxis(fades, 1, 0), jnp.moveaxis(carried...  68 us
    unnamed x297, local copies, waits for them, and re-layouts  56.7 us
    dynamic_slice x32, local copies, waits for them, and re-layouts, mixer_front(): lax.scan(advance, start, (jnp.moveaxis(fades, 1, 0), jnp.moveaxis(carried...  53.4 us
    reshape x11, local copies, waits for them, and re-layouts, shaped(): return array.reshape(count, blocks, STRETCH, HEADS, HEAD_DIM)  43.4 us
  transfers between devices with their start and end apart: 6, of which 2 were waited for; matrix products, arithmetic and copies ran while one was open for 2% of the time, Pallas kernels for 0%

commit v1 on v0

v1 whole, which is shorter than its diff:
```python
import functools
import math

import jax
import jax.numpy as jnp
from jax import lax
from jax.experimental import pallas as pl
from jax.experimental.pallas import tpu as pltpu
from jax.sharding import PartitionSpec as P

HEADS = 6
HEAD_DIM = 64
CLASSES = 1000
FREQ = 256
GRID = 64
WIDTH = 384
PAIRS = 3
LANES = 128
CHUNK = 128
TILE = 256
HALF = 256
SPAN = 120.0
HIGH = lax.Precision.HIGHEST
F32 = jnp.float32
BF16 = jnp.bfloat16
GELU_C = math.sqrt(2.0 / math.pi)


def product(left, right):
    return jnp.dot(left, right, precision=HIGH, preferred_element_type=F32)


def dot(a, b, ca=1, cb=0):
    return lax.dot_general(a, b, (((ca,), (cb,)), ((), ())), preferred_element_type=F32)


def split(x):
    high = x.astype(BF16)
    return high, (x - high.astype(F32)).astype(BF16)


def mm3(a, b, ca=1, cb=0):
    return dot(a[0], b[0], ca, cb) + dot(a[1], b[0], ca, cb) + dot(a[0], b[1], ca, cb)


def split3(x):
    high = x.astype(BF16)
    rest = x - high.astype(F32)
    middle = rest.astype(BF16)
    return high, middle, (rest - middle.astype(F32)).astype(BF16)


def mm6(a, b, ca=1, cb=0):
    terms = ((0, 0), (0, 1), (1, 0), (1, 1), (0, 2), (2, 0))
    return sum(dot(a[i], b[j], ca, cb) for i, j in reversed(terms))


def wide6(x):
    h, m, l = split3(x)
    return jnp.concatenate([h, h, m, m, h, l], axis=1)


def tall6(w):
    h, m, l = split3(w)
    return jnp.concatenate([h, m, h, m, l, h], axis=0)


def wide(x):
    high, low = split(x)
    return jnp.concatenate([high, low, high], axis=1)


def tall(w):
    high, low = split(w)
    return jnp.concatenate([high, high, low], axis=0)


def across(w):
    high, low = split(w)
    return jnp.concatenate([high, high, low], axis=1)


def lanes(x, p):
    return x[..., p * LANES : (p + 1) * LANES]


def first_half(shape):
    return lax.broadcasted_iota(jnp.int32, shape, len(shape) - 1) < HEAD_DIM


def block_diagonal(square):
    rows = lax.broadcasted_iota(jnp.int32, square.shape, 0) < HEAD_DIM
    return jnp.where(rows == first_half(square.shape), square, 0.0)


def head_mean(x):
    rows = lax.broadcasted_iota(jnp.int32, (LANES, LANES), 0) < HEAD_DIM
    ones = jnp.where(rows == first_half((LANES, LANES)), 1.0 / HEAD_DIM, 0.0).astype(BF16)
    high, low = split(x)
    return dot(
        jnp.concatenate([high, low], axis=1), jnp.concatenate([ones, ones], axis=0)
    )


def head_means(x):
    return jnp.concatenate([head_mean(lanes(x, p)) for p in range(PAIRS)], axis=1)


def stacked_heads(x):
    keep = first_half(x.shape)
    zero = jnp.zeros_like(x)
    return jnp.concatenate([jnp.where(keep, x, zero), jnp.where(keep, zero, x)], axis=0)


def merged_heads(x):
    rows = x.shape[0] // 2
    return jnp.where(first_half((rows, LANES)), x[:rows], x[rows:])


def sigmoid(x):
    return 1.0 / (1.0 + jnp.exp(-x))


def shifted(x, step):
    rows = x.shape[0]
    column = lax.broadcasted_iota(jnp.int32, x.shape, 0) % GRID
    if step == 1:
        return jnp.where(column == 0, 0.0, pltpu.roll(x, 1, 0))
    return jnp.where(column == GRID - 1, 0.0, pltpu.roll(x, rows - 1, 0))


def normalized(x):
    center = x - jnp.mean(x, axis=-1, keepdims=True)
    rate = lax.rsqrt(jnp.mean(center * center, axis=-1, keepdims=True) + 1e-06)
    return center * rate, rate


def normal_back(dhat, hat, rate):
    return rate * (
        dhat
        - jnp.mean(dhat, axis=-1, keepdims=True)
        - hat * jnp.mean(dhat * hat, axis=-1, keepdims=True)
    )


def triangle(size, upper):
    rows = lax.broadcasted_iota(jnp.int32, (size, size), 0)
    cols = lax.broadcasted_iota(jnp.int32, (size, size), 1)
    return jnp.where(cols >= rows if upper else cols <= rows, 1.0, 0.0).astype(BF16)


def running_sum(x, upper):
    tri = triangle(x.shape[0], upper)
    high = x.astype(BF16)
    rest = x - high.astype(F32)
    middle = rest.astype(BF16)
    low = (rest - middle.astype(F32)).astype(BF16)
    return dot(tri, high) + dot(tri, middle) + dot(tri, low)


def front_kernel(
    edge_ref,
    real_ref,
    tok_ref,
    top_ref,
    bot_ref,
    mod_ref,
    taps_ref,
    w_ref,
    bias_ref,
    normed_ref,
    conv_ref,
    q_ref,
    k_ref,
    v_ref,
    cum_ref,
    slope_ref,
    far_ref,
    state_ref,
    fade_ref,
    out_ref,
    w3_ref,
    st_ref,
    dev_ref,
):
    image = pl.program_id(0)
    length = tok_ref.shape[0]

    @pl.when(image == 0)
    def _():
        w3_ref[...] = tall6(w_ref[...])

    shift = mod_ref[0:1, :]
    scale = 1.0 + mod_ref[1:2, :]

    def modulated(x):
        return normalized(x)[0] * scale + shift

    normed_ref[0:GRID, :] = jnp.where(edge_ref[0] > 0, 0.0, modulated(top_ref[...]))
    normed_ref[pl.ds(length + GRID, GRID), :] = jnp.where(
        edge_ref[1] > 0, 0.0, modulated(bot_ref[...])
    )

    def norm_step(i, carry):
        start = pl.multiple_of(i * TILE, TILE)
        normed_ref[pl.ds(start + GRID, TILE), :] = modulated(tok_ref[pl.ds(start, TILE), :])
        return carry

    lax.fori_loop(0, length // TILE, norm_step, 0)
    st_ref[...] = jnp.zeros_like(st_ref)
    dev_ref[...] = jnp.zeros_like(dev_ref)

    def tile_step(i, carry):
        start = pl.multiple_of(i * TILE, TILE)
        rows = [normed_ref[pl.ds(start + a * GRID, TILE), :] for a in range(3)]
        parts = [
            sum(taps_ref[3 * a + b : 3 * a + b + 1, :] * rows[a] for a in range(3))
            for b in range(3)
        ]
        conv = shifted(parts[0], 1) + parts[1] + shifted(parts[2], -1)
        conv_ref[pl.ds(start, TILE), :] = conv
        hidden = conv * sigmoid(conv)
        proj = dot(wide6(hidden), w3_ref[...])
        keep = (
            lax.broadcasted_iota(jnp.int32, (TILE, WIDTH), 0) + start < real_ref[image]
        )
        q = proj[:, :WIDTH]
        k = jnp.where(keep, proj[:, WIDTH : 2 * WIDTH], 0.0)
        v = jnp.where(keep, proj[:, 2 * WIDTH : 3 * WIDTH], 0.0)
        x = proj[:, 3 * WIDTH :] + bias_ref[...]
        small = jnp.exp(-jnp.abs(x))
        gates = jnp.where(keep, (jnp.minimum(x, 0.0) - jnp.log1p(small)) * (1.0 / 16.0), 0.0)
        slope = jnp.where(x >= 0, small, 1.0) / (1.0 + small)
        slope_ref[pl.ds(start, TILE), :] = jnp.where(keep, slope * (1.0 / 16.0), 0.0)
        q_ref[pl.ds(start, TILE), :] = q
        k_ref[pl.ds(start, TILE), :] = k
        v_ref[pl.ds(start, TILE), :] = v
        for c in range(TILE // CHUNK):
            at = slice(c * CHUNK, (c + 1) * CHUNK)
            chunk = i * (TILE // CHUNK) + c
            cum = running_sum(gates[at], False)
            cum_ref[pl.ds(start + c * CHUNK, CHUNK), :] = cum
            final = cum[CHUNK - 1 : CHUNK, :]
            dev = dev_ref[0:1, :]
            far_ref[pl.ds(start + c * CHUNK, CHUNK), :] = q[at] * jnp.exp(cum + dev)
            fade_ref[chunk] = jnp.broadcast_to(jnp.exp(dev), (8, WIDTH))
            kd = k[at] * jnp.exp(final - cum)
            factor = jnp.exp(final)
            for p in range(PAIRS):
                state_ref[chunk, p] = st_ref[p]
                update = mm3(split(lanes(v[at], p)), split(lanes(kd, p)), 0, 0)
                st_ref[p] = lanes(factor, p) * st_ref[p] + block_diagonal(update)
            dev_ref[...] = dev_ref[...] + final
        return carry

    lax.fori_loop(0, length // TILE, tile_step, 0)
    for p in range(PAIRS):
        out_ref[p, 0:HEAD_DIM, :] = st_ref[p, 0:HEAD_DIM, :] + st_ref[p, HEAD_DIM:, :]
        out_ref[p, HEAD_DIM:, :] = jnp.exp(lanes(dev_ref[...], p))


def exact_scores(q_ref, k_ref, cum_ref, base, s_ref):
    q = q_ref[pl.ds(base, CHUNK), :]
    cum = cum_ref[pl.ds(base, CHUNK), :]
    s_ref[...] = jnp.zeros_like(s_ref)

    def step(j, carry):
        key = k_ref[pl.ds(base + j, 1), :]
        weight = jnp.exp(jnp.minimum(cum - cum_ref[pl.ds(base + j, 1), :], 0.0))
        terms = q * key * weight
        for p in range(PAIRS):
            column = jnp.sum(stacked_heads(lanes(terms, p)), axis=1, keepdims=True)
            at = lax.broadcasted_iota(jnp.int32, (2 * CHUNK, CHUNK), 1) == j
            s_ref[p] = jnp.where(at, column, s_ref[p])
        return carry

    lax.fori_loop(0, CHUNK, step, 0)


def causal_two():
    rows = lax.broadcasted_iota(jnp.int32, (2 * CHUNK, CHUNK), 0) % CHUNK
    return rows >= lax.broadcasted_iota(jnp.int32, (2 * CHUNK, CHUNK), 1)


def inner_kernel(
    q_ref, k_ref, v_ref, cum_ref, state_ref, normed_ref, gate_ref, o_ref, s_ref, gp_ref, w3_ref, tmp_ref
):
    @pl.when((pl.program_id(0) == 0) & (pl.program_id(1) == 0))
    def _():
        w3_ref[...] = tall(gate_ref[...])

    start = pl.multiple_of(pl.program_id(1) * TILE + GRID, GRID)
    gp_ref[...] = dot(wide(normed_ref[pl.ds(start, TILE), :]), w3_ref[...])
    mask = causal_two()
    for c in range(TILE // CHUNK):
        base = c * CHUNK
        at = slice(base, base + CHUNK)
        q = q_ref[at, :]
        k = k_ref[at, :]
        cum = cum_ref[at, :]
        final = cum[CHUNK - 1 : CHUNK, :]
        wild = jnp.max(-final) > SPAN
        middle = 0.5 * final
        qf = split3(q * jnp.exp(cum - middle))
        kf = split3(k * jnp.exp(middle - cum))
        for p in range(PAIRS):
            qp = tuple(stacked_heads(lanes(part, p)) for part in qf)
            kp = tuple(lanes(part, p) for part in kf)
            tmp_ref[p] = mm6(qp, kp, 1, 1)

        @pl.when(wild)
        def _():
            exact_scores(q_ref, k_ref, cum_ref, base, tmp_ref)

        qd = q * jnp.exp(cum)
        for p in range(PAIRS):
            s = jnp.where(mask, tmp_ref[p], 0.0)
            s_ref[c, p] = s
            inner = merged_heads(mm3(split(s), split(lanes(v_ref[at, :], p))))
            outer = mm3(split(lanes(qd, p)), split(state_ref[c, p]), 1, 1)
            o_ref[at, p * LANES : (p + 1) * LANES] = inner + outer


def tail_kernel(
    o_ref,
    far_ref,
    tok_ref,
    normed_ref,
    gp_ref,
    cot_ref,
    st_ref,
    mod_ref,
    out_w_ref,
    gate_w_ref,
    up_ref,
    down_ref,
    block_ref,
    dmid_ref,
    datt_ref,
    dnorm_ref,
    g_out_ref,
    g_gate_ref,
    g_up_ref,
    g_down_ref,
    dmod_ref,
    dst_ref,
    o3_ref,
    ot3_ref,
    gt3_ref,
    u3_ref,
    ut_ref,
    d_ref,
    dt3_ref,
    gd_ref,
    mlp_ref,
    dsec_ref,
):
    image, tile = pl.program_id(0), pl.program_id(1)
    blocks = u3_ref.shape[0]

    @pl.when((image == 0) & (tile == 0))
    def _():
        o3_ref[...] = tall(out_w_ref[...])
        ot3_ref[...] = across(out_w_ref[...])
        gt3_ref[...] = across(gate_w_ref[...])
        g_out_ref[...] = jnp.zeros_like(g_out_ref)
        g_gate_ref[...] = jnp.zeros_like(g_gate_ref)
        g_up_ref[...] = jnp.zeros_like(g_up_ref)
        gd_ref[...] = jnp.zeros_like(gd_ref)
        for j in range(blocks):
            up = up_ref[:, j * HALF : (j + 1) * HALF]
            u3_ref[j] = tall(up)
            ut_ref[j] = jnp.concatenate(split(up), axis=0)
            down = down_ref[j * HALF : (j + 1) * HALF, :]
            d_ref[j] = jnp.concatenate(split(down), axis=0)
            dt3_ref[j] = across(down)

    @pl.when(tile == 0)
    def _():
        dmod_ref[...] = jnp.zeros_like(dmod_ref)
        dst_ref[...] = jnp.zeros_like(dst_ref)

    gate_a = mod_ref[2:3, :]
    shift_b = mod_ref[3:4, :]
    scale_b = 1.0 + mod_ref[4:5, :]
    gate_b = mod_ref[5:6, :]
    far = split(far_ref[...])
    att = o_ref[...] + jnp.concatenate(
        [
            mm3(tuple(lanes(part, p) for part in far), split(st_ref[p]), 1, 1)
            for p in range(PAIRS)
        ],
        axis=1,
    )
    rate = lax.rsqrt(head_means(att * att) + 1e-05)
    unit = att * rate
    gp = gp_ref[...]
    sig = sigmoid(gp)
    gate = gp * sig
    y = unit * gate
    y_pair = split(y)
    branch = dot(jnp.concatenate([y_pair[0], y_pair[1], y_pair[0]], axis=1), o3_ref[...])
    middle = tok_ref[...] + gate_a * branch
    hat, rate_b = normalized(middle)
    second = hat * scale_b + shift_b
    second3 = wide(second)
    cot = cot_ref[...]
    dmlp = cot * gate_b
    dmlp3 = wide(dmlp)
    second_t = split(second.T)
    dmlp_t = split(dmlp.T)
    mlp_ref[...] = jnp.zeros_like(mlp_ref)
    dsec_ref[...] = jnp.zeros_like(dsec_ref)

    def step(j, carry):
        u = dot(second3, u3_ref[j])
        square = u * u
        th = jnp.tanh(GELU_C * (u + 0.044715 * u * square))
        act = 0.5 * u * (1.0 + th)
        slope = 0.5 * (1.0 + th) + 0.5 * u * (1.0 - th * th) * (
            GELU_C * (1.0 + 3.0 * 0.044715 * square)
        )
        act_pair = split(act)
        down = (d_ref[j, 0:HALF, :], d_ref[j, HALF:, :])
        mlp_ref[...] += mm3(act_pair, down)
        du = split(dot(dmlp3, dt3_ref[j], 1, 1) * slope)
        up = (ut_ref[j, 0:WIDTH, :], ut_ref[j, WIDTH:, :])
        dsec_ref[...] += mm3(du, up, 1, 1)
        at = pl.ds(pl.multiple_of(j * HALF, HALF), HALF)
        g_up_ref[:, at] += mm3(second_t, du)
        gd_ref[j] += mm3(dmlp_t, act_pair)
        return carry

    lax.fori_loop(0, blocks, step, 0)

    mlp = mlp_ref[...]
    block_ref[...] = middle + gate_b * mlp
    dsec = dsec_ref[...]
    dmid = cot + normal_back(dsec * scale_b, hat, rate_b)
    dmid_ref[...] = dmid

    def total(x):
        return jnp.sum(x, axis=0, keepdims=True)

    dmod_ref[2:3, :] += total(dmid * branch)
    dmod_ref[3:4, :] += total(dsec)
    dmod_ref[4:5, :] += total(dsec * hat)
    dmod_ref[5:6, :] += total(cot * mlp)
    dbranch = dmid * gate_a
    dbr = split(dbranch)
    dy = dot(jnp.concatenate([dbr[0], dbr[1], dbr[0]], axis=1), ot3_ref[...], 1, 1)
    g_out_ref[...] += mm3(y_pair, dbr, 0, 0)
    dunit = dy * gate
    dgp = (dy * unit) * (sig * (1.0 + gp * (1.0 - sig)))
    datt = rate * (dunit - unit * head_means(dunit * unit))
    datt_ref[...] = datt
    dg = split(dgp)
    dnorm_ref[...] = dot(jnp.concatenate([dg[0], dg[1], dg[0]], axis=1), gt3_ref[...], 1, 1)
    start = pl.multiple_of(tile * TILE + GRID, GRID)
    g_gate_ref[...] += mm3(split(normed_ref[pl.ds(start, TILE), :]), dg, 0, 0)
    da = split(datt)
    for p in range(PAIRS):
        grad = mm3(
            tuple(lanes(part, p) for part in da), tuple(lanes(part, p) for part in far), 0, 0
        )
        dst_ref[p] += block_diagonal(grad)

    @pl.when((image == pl.num_programs(0) - 1) & (tile == pl.num_programs(1) - 1))
    def _():
        for j in range(blocks):
            g_down_ref[j * HALF : (j + 1) * HALF, :] = gd_ref[j].T


def exact_back(q_ref, k_ref, cum_ref, ds_ref, base, dq_ref, dk_ref):
    q = q_ref[pl.ds(base, CHUNK), :]
    cum = cum_ref[pl.ds(base, CHUNK), :]
    dq_ref[...] = jnp.zeros_like(dq_ref)

    def step(j, carry):
        key = k_ref[pl.ds(base + j, 1), :]
        weight = jnp.exp(jnp.minimum(cum - cum_ref[pl.ds(base + j, 1), :], 0.0))
        at = lax.broadcasted_iota(jnp.int32, (2 * CHUNK, CHUNK), 1) == j
        columns = []
        for p in range(PAIRS):
            column = jnp.sum(jnp.where(at, ds_ref[p], 0.0), axis=1, keepdims=True)
            columns.append(merged_heads(jnp.broadcast_to(column, (2 * CHUNK, LANES))))
        ds = jnp.concatenate(columns, axis=1) * weight
        dq_ref[...] += ds * key
        dk_ref[pl.ds(j, 1), :] = jnp.sum(ds * q, axis=0, keepdims=True)
        return carry

    lax.fori_loop(0, CHUNK, step, 0)


def inner_back_kernel(
    q_ref,
    k_ref,
    v_ref,
    cum_ref,
    datt_ref,
    s_ref,
    state_ref,
    fade_ref,
    st_ref,
    dq_ref,
    dk_ref,
    dv_ref,
    full_ref,
    ds_ref,
    dqi_ref,
    dki_ref,
):
    mask = causal_two()
    for c in range(TILE // CHUNK):
        base = c * CHUNK
        at = slice(base, base + CHUNK)
        q = q_ref[at, :]
        k = k_ref[at, :]
        cum = cum_ref[at, :]
        final = cum[CHUNK - 1 : CHUNK, :]
        wild = jnp.max(-final) > SPAN
        middle = 0.5 * final
        eq = jnp.exp(cum - middle)
        ek = jnp.exp(middle - cum)
        qf = split(q * eq)
        kf = split(k * ek)
        da = split3(datt_ref[at, :])
        vs = split3(v_ref[at, :])
        for p in range(PAIRS):
            da2 = tuple(stacked_heads(lanes(part, p)) for part in da)
            vp = tuple(lanes(part, p) for part in vs)
            ds = jnp.where(mask, mm6(da2, vp, 1, 1), 0.0)
            ds_ref[p] = ds
            ds2 = split(ds)
            kp = tuple(lanes(part, p) for part in kf)
            qp = tuple(lanes(part, p) for part in qf)
            dqi_ref[:, p * LANES : (p + 1) * LANES] = merged_heads(mm3(ds2, kp)) * lanes(eq, p)
            q2 = tuple(stacked_heads(part) for part in qp)
            dki_ref[:, p * LANES : (p + 1) * LANES] = mm3(ds2, q2, 0, 0) * lanes(ek, p)
            s2 = split(s_ref[c, p])
            dv_ref[at, p * LANES : (p + 1) * LANES] = mm3(s2, da2, 0, 0)

        @pl.when(wild)
        def _():
            exact_back(q_ref, k_ref, cum_ref, ds_ref, base, dqi_ref, dki_ref)

        grow = jnp.exp(cum)
        for p in range(PAIRS):
            full = state_ref[c, p] + lanes(fade_ref[c, 0:1, :], p) * st_ref[p]
            full_ref[c, p] = full
            outer = mm3(tuple(lanes(part, p) for part in da), split(full))
            dq_ref[at, p * LANES : (p + 1) * LANES] = (
                dqi_ref[:, p * LANES : (p + 1) * LANES] + outer * lanes(grow, p)
            )
        dk_ref[at, :] = dki_ref[...]


def state_back_kernel(
    real_ref,
    q_ref,
    k_ref,
    v_ref,
    cum_ref,
    slope_ref,
    conv_ref,
    datt_ref,
    dq_ref,
    dk_ref,
    dv_ref,
    full_ref,
    dout_ref,
    w_ref,
    proj_ref,
    dconv_ref,
    dbias_ref,
    wt3_ref,
    dst_ref,
):
    image, turn = pl.program_id(0), pl.program_id(1)
    tile = pl.num_programs(1) - 1 - turn

    @pl.when((image == 0) & (turn == 0))
    def _():
        wt3_ref[...] = across(w_ref[...])
        dbias_ref[...] = jnp.zeros_like(dbias_ref)

    @pl.when(turn == 0)
    def _():
        dst_ref[...] = dout_ref[...]

    keep = (
        lax.broadcasted_iota(jnp.int32, (CHUNK, WIDTH), 0) + tile * TILE
    )
    for c in reversed(range(TILE // CHUNK)):
        at = slice(c * CHUNK, (c + 1) * CHUNK)
        q = q_ref[at, :]
        k = k_ref[at, :]
        cum = cum_ref[at, :]
        final = cum[CHUNK - 1 : CHUNK, :]
        late = jnp.exp(final - cum)
        kd = k * late
        v = v_ref[at, :]
        qd = split(q * jnp.exp(cum))
        da = split(datt_ref[at, :])
        factor = jnp.exp(final)
        dk_parts, dv_parts, cross = [], [], []
        for p in range(PAIRS):
            old = dst_ref[p]
            pair = split(old)
            dk_parts.append(mm3(split(lanes(v, p)), pair))
            dv_parts.append(mm3(split(lanes(kd, p)), pair, 1, 1))
            leaving = lanes(factor, p) * full_ref[c, p] + block_diagonal(
                mm3(split(lanes(v, p)), split(lanes(kd, p)), 0, 0)
            )
            cross.append(jnp.sum(leaving * old, axis=0, keepdims=True))
            update = mm3(
                tuple(lanes(part, p) for part in da), tuple(lanes(part, p) for part in qd), 0, 0
            )
            dst_ref[p] = lanes(factor, p) * old + block_diagonal(update)
        dq = dq_ref[at, :]
        dk = dk_ref[at, :] + jnp.concatenate(dk_parts, axis=1) * late
        dv = dv_ref[at, :] + jnp.concatenate(dv_parts, axis=1)
        dgates = running_sum(q * dq - k * dk, True) + jnp.concatenate(cross, axis=1)
        dx = dgates * slope_ref[at, :]
        real = keep + c * CHUNK < real_ref[image]
        dk = jnp.where(real, dk, 0.0)
        dv = jnp.where(real, dv, 0.0)
        dbias_ref[...] += jnp.sum(dx.reshape(CHUNK // 8, 8, WIDTH), axis=0)
        proj_ref[at, 0:WIDTH] = dq
        proj_ref[at, WIDTH : 2 * WIDTH] = dk
        proj_ref[at, 2 * WIDTH : 3 * WIDTH] = dv
        proj_ref[at, 3 * WIDTH :] = dx
    dhidden = dot(wide(proj_ref[...]), wt3_ref[...], 1, 1)
    conv = conv_ref[...]
    sig = sigmoid(conv)
    dconv_ref[...] = dhidden * (sig * (1.0 + conv * (1.0 - sig)))


def weight_kernel(conv_ref, proj_ref, g_ref):
    @pl.when((pl.program_id(0) == 0) & (pl.program_id(1) == 0))
    def _():
        g_ref[...] = jnp.zeros_like(g_ref)

    conv = conv_ref[...]
    hidden = split((conv * sigmoid(conv)).T)
    for j in range(4):
        at = slice(j * WIDTH, (j + 1) * WIDTH)
        g_ref[:, at] += mm3(hidden, split(proj_ref[:, at]))


def front_back_kernel(
    tok_ref,
    normed_ref,
    dconv_ref,
    top_ref,
    bot_ref,
    dnorm_ref,
    dmid_ref,
    mod_ref,
    taps_ref,
    grad_ref,
    dmod_ref,
    dtaps_ref,
    pad_ref,
):
    length = tok_ref.shape[0]

    @pl.when(pl.program_id(0) == 0)
    def _():
        dtaps_ref[...] = jnp.zeros_like(dtaps_ref)

    dmod_ref[...] = jnp.zeros_like(dmod_ref)
    pad_ref[0:GRID, :] = top_ref[...]
    pad_ref[pl.ds(length + GRID, GRID), :] = bot_ref[...]
    pad_ref[pl.ds(GRID, length), :] = dconv_ref[...]
    scale = 1.0 + mod_ref[1:2, :]

    def eights(x):
        return jnp.sum(x.reshape(x.shape[0] // 8, 8, WIDTH), axis=0)

    def step(i, carry):
        start = pl.multiple_of(i * TILE, TILE)
        rows = [pad_ref[pl.ds(start + (2 - a) * GRID, TILE), :] for a in range(3)]
        parts = [
            sum(taps_ref[3 * a + b : 3 * a + b + 1, :] * rows[a] for a in range(3))
            for b in range(3)
        ]
        dn = (
            shifted(parts[0], -1)
            + parts[1]
            + shifted(parts[2], 1)
            + dnorm_ref[pl.ds(start, TILE), :]
        )
        hat, rate = normalized(tok_ref[pl.ds(start, TILE), :])
        grad_ref[pl.ds(start, TILE), :] = dmid_ref[pl.ds(start, TILE), :] + normal_back(
            dn * scale, hat, rate
        )
        dmod_ref[0:1, :] += jnp.sum(dn, axis=0, keepdims=True)
        dmod_ref[1:2, :] += jnp.sum(dn * hat, axis=0, keepdims=True)
        own = rows[1]
        moved = [shifted(own, -1), own, shifted(own, 1)]
        for a in range(3):
            near = normed_ref[pl.ds(start + a * GRID, TILE), :]
            for b in range(3):
                dtaps_ref[3 * a + b] += eights(moved[b] * near)
        return carry

    lax.fori_loop(0, length // TILE, step, 0)


def call(kernel, grid, ins, outs, scratch, flops=0, moved=0, prefetch=0, limit=60):
    return pl.pallas_call(
        kernel,
        grid_spec=pltpu.PrefetchScalarGridSpec(
            num_scalar_prefetch=prefetch,
            grid=grid,
            in_specs=ins,
            out_specs=[spec for spec, _ in outs],
            scratch_shapes=scratch,
        ),
        out_shape=[jax.ShapeDtypeStruct(shape, F32) for _, shape in outs],
        compiler_params=pltpu.CompilerParams(vmem_limit_bytes=limit * 1024 * 1024),
        cost_estimate=pl.CostEstimate(flops=flops, bytes_accessed=moved, transcendentals=0),
    )


def whole(shape):
    zeros = (0,) * len(shape)
    return pl.BlockSpec(shape, lambda *_: zeros, pipeline_mode=pl.Buffered(1))


def per_image(shape):
    zeros = (0,) * len(shape)
    return pl.BlockSpec((None,) + shape, lambda n, *_: (n,) + zeros)


def time_features(timesteps):
    half = FREQ // 2
    freqs = jnp.exp(-math.log(10000.0) * jnp.arange(half, dtype=F32) / half)
    angles = timesteps.astype(F32)[:, None] * freqs[None, :]
    return jnp.concatenate([jnp.cos(angles), jnp.sin(angles)], axis=1)


def expanded(compact):
    keep = jnp.arange(LANES) < HEAD_DIM
    zero = jnp.zeros_like(compact)
    return jnp.concatenate(
        [jnp.where(keep, compact, zero), jnp.where(keep, zero, compact)], axis=-2
    )


def chained(message, axis, backward):
    size = lax.axis_size(axis)
    total = jnp.zeros_like(message[..., :HEAD_DIM, :])
    got = []
    for far in range(1, size):
        pairs = [(i, i + far) for i in range(size - far)]
        if backward:
            pairs = [(j, i) for i, j in pairs]
        got.append(lax.ppermute(message, axis, pairs))
    for part in reversed(got):
        total = part[..., :HEAD_DIM, :] + part[..., HEAD_DIM : HEAD_DIM + 1, :] * total
    return expanded(total)


def body(
    tokens,
    valid_mask,
    timesteps,
    class_ids,
    time_first,
    time_second,
    class_table,
    ada_weight,
    ada_bias,
    conv_taps,
    query_proj,
    key_proj,
    value_proj,
    decay_down,
    decay_up,
    decay_bias,
    gate_proj,
    out_proj,
    mlp_up,
    mlp_down,
    cotangent,
):
    count, length, width = tokens.shape
    size, mine = lax.axis_size("seq"), lax.axis_index("seq")
    hidden_units = mlp_up.shape[1]
    tiles, chunks = length // TILE, length // CHUNK
    per_tile = TILE // CHUNK
    blocks = hidden_units // HALF
    up_pairs = [(i, i + 1) for i in range(size - 1)]
    down_pairs = [(j, i) for i, j in up_pairs]

    def borders(x, before_of, after_of):
        return (
            lax.ppermute(before_of(x), "seq", up_pairs),
            lax.ppermute(after_of(x), "seq", down_pairs),
        )

    above, below = borders(tokens, lambda x: x[:, length - GRID :], lambda x: x[:, :GRID])

    features = time_features(timesteps)
    first = product(features, time_first)
    embed = product(jax.nn.silu(first), time_second)
    onehot = (class_ids[:, None] == jnp.arange(CLASSES, dtype=jnp.int32)[None, :]).astype(F32)
    embed = embed + product(onehot, class_table)
    modul = (product(jax.nn.silu(embed), ada_weight) + ada_bias).reshape(count, 6, width)

    real = jnp.sum(valid_mask, axis=1, dtype=jnp.int32)
    edge = jnp.stack([mine == 0, mine == size - 1]).astype(jnp.int32)
    weights = jnp.concatenate(
        [query_proj * HEAD_DIM ** (-0.5), key_proj, value_proj, product(decay_down, decay_up)],
        axis=1,
    )
    row = (length, width)
    image_row = (per_image(row), (count,) + row)
    dense = 2 * 3 * count * length * width
    (
        normed,
        conv,
        query,
        keys,
        values,
        cumul,
        slope,
        far,
        states,
        fades,
        message,
    ) = call(
        front_kernel,
        (count,),
        [
            per_image(row),
            per_image((GRID, width)),
            per_image((GRID, width)),
            per_image((6, width)),
            whole((9, width)),
            whole((width, 4 * width)),
            whole((1, width)),
        ],
        [(per_image((length + 2 * GRID, width)), (count, length + 2 * GRID, width))]
        + [image_row] * 7
        + [
            (
                per_image((chunks, PAIRS, LANES, LANES)),
                (count, chunks, PAIRS, LANES, LANES),
            ),
            (per_image((chunks, 8, width)), (count, chunks, 8, width)),
            (per_image((PAIRS, HEAD_DIM + 8, LANES)), (count, PAIRS, HEAD_DIM + 8, LANES)),
        ],
        [
            pltpu.VMEM((6 * width, 4 * width), BF16),
            pltpu.VMEM((PAIRS, LANES, LANES), F32),
            pltpu.VMEM((8, width), F32),
        ],
        flops=dense * 4 * width,
        moved=4 * count * length * width * 10,
        prefetch=2,
    )(edge, real, tokens, above, below, modul, conv_taps, weights, decay_bias[None])

    def tiled(shape=(TILE, width)):
        return pl.BlockSpec((None,) + shape, lambda n, i: (n, i, 0))

    tile_row = (tiled(), (count,) + row)
    pair_spec = pl.BlockSpec(
        (None, per_tile, PAIRS, LANES, LANES), lambda n, i: (n, i, 0, 0, 0)
    )
    state_spec = pl.BlockSpec((None, PAIRS, LANES, LANES), lambda n, i: (n, 0, 0, 0))
    score_shape = (count, chunks, PAIRS, 2 * CHUNK, CHUNK)
    score_spec = pl.BlockSpec(
        (None, per_tile, PAIRS, 2 * CHUNK, CHUNK), lambda n, i: (n, i, 0, 0, 0)
    )
    normed_spec = per_image((length + 2 * GRID, width))
    state_in = chained(message, "seq", False)
    inner, scores, gate_in = call(
        inner_kernel,
        (count, tiles),
        [tiled()] * 4 + [pair_spec, normed_spec, whole((width, width))],
        [tile_row, (score_spec, score_shape), tile_row],
        [pltpu.VMEM((3 * width, width), BF16), pltpu.VMEM((PAIRS, 2 * CHUNK, CHUNK), F32)],
        flops=dense * 2 * width,
        moved=4 * count * length * width * 9,
    )(query, keys, values, cumul, states, normed, gate_proj)

    square, up_shape, down_shape = (width, width), (width, hidden_units), (hidden_units, width)
    mod_spec = per_image((6, width))
    dmod_spec = per_image((8, width))
    (
        block_out,
        dmid,
        datt,
        dnorm,
        g_out,
        g_gate,
        g_up,
        g_down,
        dmod_tail,
        dstate,
    ) = call(
        tail_kernel,
        (count, tiles),
        [tiled(), tiled(), tiled(), normed_spec, tiled(), tiled(), state_spec, mod_spec]
        + [whole(square), whole(square), whole(up_shape), whole(down_shape)],
        [tile_row] * 4
        + [(whole(shape), shape) for shape in (square, square, up_shape, down_shape)]
        + [
            (dmod_spec, (count, 8, width)),
            (state_spec, (count, PAIRS, LANES, LANES)),
        ],
        [
            pltpu.VMEM((3 * width, width), BF16),
            pltpu.VMEM((width, 3 * width), BF16),
            pltpu.VMEM((width, 3 * width), BF16),
            pltpu.VMEM((blocks, 3 * width, HALF), BF16),
            pltpu.VMEM((blocks, 2 * width, HALF), BF16),
            pltpu.VMEM((blocks, 2 * HALF, width), BF16),
            pltpu.VMEM((blocks, HALF, 3 * width), BF16),
            pltpu.VMEM((blocks, width, HALF), F32),
            pltpu.VMEM((TILE, width), F32),
            pltpu.VMEM((TILE, width), F32),
        ],
        flops=dense * 3 * (2 * hidden_units + 2 * width),
        moved=4 * count * length * width * 12,
    )(
        inner,
        far,
        tokens,
        normed,
        gate_in,
        cotangent,
        state_in,
        modul,
        out_proj,
        gate_proj,
        mlp_up,
        mlp_down,
    )

    dcompact = dstate[:, :, :HEAD_DIM] + dstate[:, :, HEAD_DIM:]
    d_message = jnp.concatenate([dcompact, message[:, :, HEAD_DIM:]], axis=2)
    d_outgoing = chained(d_message, "seq", True)
    fade_spec = pl.BlockSpec((None, per_tile, 8, width), lambda n, i: (n, i, 0, 0))
    dquery, dkeys, dvalues, full = call(
        inner_back_kernel,
        (count, tiles),
        [tiled()] * 5 + [score_spec, pair_spec, fade_spec, state_spec],
        [tile_row] * 3 + [(pair_spec, (count, chunks, PAIRS, LANES, LANES))],
        [
            pltpu.VMEM((PAIRS, 2 * CHUNK, CHUNK), F32),
            pltpu.VMEM((CHUNK, width), F32),
            pltpu.VMEM((CHUNK, width), F32),
        ],
        flops=dense * 2 * width,
        moved=4 * count * length * width * 12,
    )(query, keys, values, cumul, datt, scores, states, fades, state_in)

    def turned(shape=(TILE, width)):
        return pl.BlockSpec((None,) + shape, lambda n, i, *_: (n, tiles - 1 - i, 0))

    dproj, dconv, dbias = call(
        state_back_kernel,
        (count, tiles),
        [turned()] * 10
        + [
            pl.BlockSpec(
                (None, per_tile, PAIRS, LANES, LANES),
                lambda n, i, *_: (n, tiles - 1 - i, 0, 0, 0),
            ),
            pl.BlockSpec((None, PAIRS, LANES, LANES), lambda n, i, *_: (n, 0, 0, 0)),
            whole((width, 4 * width)),
        ],
        [
            (turned((TILE, 4 * width)), (count, length, 4 * width)),
            (turned(), (count,) + row),
            (whole((8, width)), (8, width)),
        ],
        [
            pltpu.VMEM((width, 3 * 4 * width), BF16),
            pltpu.VMEM((PAIRS, LANES, LANES), F32),
        ],
        flops=dense * 5 * width,
        moved=4 * count * length * width * 16,
        prefetch=1,
    )(
        real,
        query,
        keys,
        values,
        cumul,
        slope,
        conv,
        datt,
        dquery,
        dkeys,
        dvalues,
        full,
        d_outgoing,
        weights,
    )

    d_above, d_below = borders(dconv, lambda x: x[:, length - GRID :], lambda x: x[:, :GRID])
    (g_weights,) = call(
        weight_kernel,
        (count, tiles),
        [tiled(), tiled((TILE, 4 * width))],
        [(whole((width, 4 * width)), (width, 4 * width))],
        [],
        flops=dense * 4 * width,
        moved=4 * count * length * width * 7,
    )(conv, dproj)

    tokens_grad, dmod_front, dtaps = call(
        front_back_kernel,
        (count,),
        [
            per_image(row),
            per_image((length + 2 * GRID, width)),
            per_image(row),
            per_image((GRID, width)),
            per_image((GRID, width)),
            per_image(row),
            per_image(row),
            per_image((6, width)),
            whole((9, width)),
        ],
        [
            image_row,
            (per_image((8, width)), (count, 8, width)),
            (whole((9, 8, width)), (9, 8, width)),
        ],
        [pltpu.VMEM((length + 2 * GRID, width), F32)],
        flops=count * length * width * 100,
        moved=4 * count * length * width * 6,
    )(tokens, normed, dconv, d_above, d_below, dnorm, dmid, modul, conv_taps)

    g_query, g_key, g_value, g_decay = jnp.split(g_weights, 4, axis=1)
    g_query = g_query * HEAD_DIM ** (-0.5)
    g_decay_down = product(g_decay, decay_up.T)
    g_decay_up = product(decay_down.T, g_decay)
    both = ("img", "seq")
    g_gate, g_out, g_up, g_down = lax.psum((g_gate, g_out, g_up, g_down), both)
    late = lax.psum(
        (
            jnp.sum(dtaps, axis=1),
            g_query,
            g_key,
            g_value,
            g_decay_down,
            g_decay_up,
            jnp.sum(dbias, axis=0),
        ),
        both,
    )

    dmod = dmod_front[:, :6].reshape(count, 6 * width) + dmod_tail[:, :6].reshape(count, 6 * width)
    images = lax.all_gather(
        jnp.concatenate([lax.psum(dmod, "seq"), features, first, embed], axis=1), "img", tiled=True
    )
    ids = lax.all_gather(class_ids, "img", tiled=True)
    dmod = images[:, : 6 * width]
    features = images[:, 6 * width : 6 * width + FREQ]
    first = images[:, 6 * width + FREQ : 7 * width + FREQ]
    embed = images[:, 7 * width + FREQ :]
    g_ada_weight = product(jax.nn.silu(embed).T, dmod)
    g_ada_bias = jnp.sum(dmod, axis=0)

    def silu_back(x, grad):
        sig = jax.nn.sigmoid(x)
        return grad * (sig * (1.0 + x * (1.0 - sig)))

    dembed = silu_back(embed, product(dmod, ada_weight.T))
    hot = (ids[None, :] == jnp.arange(CLASSES, dtype=jnp.int32)[:, None]).astype(F32)
    g_class_table = product(hot, dembed)
    g_time_second = product(jax.nn.silu(first).T, dembed)
    dfirst = silu_back(first, product(dembed, time_second.T))
    g_time_first = product(features.T, dfirst)
    return (
        block_out,
        tokens_grad,
        g_time_first,
        g_time_second,
        g_class_table,
        g_ada_weight,
        g_ada_bias,
        late[0],
        late[1],
        late[2],
        late[3],
        late[4],
        late[5],
        late[6],
        g_gate,
        g_out,
        g_up,
        g_down,
    )


def solution(mesh):
    image, shared = P("img", "seq", None), P()
    return jax.shard_map(
        body,
        mesh=mesh,
        in_specs=(image, P("img", "seq"), P("img"), P("img")) + (shared,) * 16 + (image,),
        out_specs=(image, image) + (shared,) * 16,
        check_vma=False,
    )
```

time: 1700 us -> 404 us (0.24)
  other arithmetic: 566 us -> 16.3 us
  local copies, waits for them, and re-layouts: 415 us -> 20.5 us
  waiting for transfers between devices: 386 us -> 45.4 us
  matrix products: 264 us -> 27.2 us
  Pallas kernels: 0 us -> 158 us
  blocking collectives: 28.5 us -> 91 us
    reduce_sum x29 -> x4, other arithmetic: 400 us -> 5.04 us  [the longest x1 1.58 us: body(): g_ada_bias = jnp.sum(dmod, axis=0)]
    psum x2 -> x1, waiting for transfers between devices: 386 us -> 45.3 us  [body(): lax.psum((jnp.sum(dtaps, axis=1), g_query, g_key, g_value, g_decay_down,...]
    dot_general x42 -> x13, matrix products: 264 us -> 27.2 us  [product(): return jnp.dot(left, right, precision=HIGH, preferred_element_type=F32)]
    pallas_call x0 -> x7, Pallas kernels: none -> 158 us  [the longest x1 71 us: body(): call(tail_kernel, (count, tiles), [tiled(), tiled(), tiled(), normed_spec...]
    mul x62 -> x2, local copies, waits for them, and re-layouts: 99.3 us -> 0.01 us  [the longest x1 0.01 us: body(): embed = product(jax.nn.silu(first), time_second)]
    dynamic_update_slice x64 -> x0, local copies, waits for them, and re-layouts: 68 us -> none  [mixer_front(): lax.scan(advance, start, (jnp.moveaxis(fades, 1, 0), jnp.moveaxis(carried...]
    reshape x15 -> x1, local copies, waits for them, and re-layouts: 62.1 us -> 0.6 us  [body(): (product(jax.nn.silu(embed), ada_weight) + ada_bias).reshape(count, 6, wi...]
    dynamic_slice x32 -> x0, local copies, waits for them, and re-layouts: 53.4 us -> none  [mixer_front(): lax.scan(advance, start, (jnp.moveaxis(fades, 1, 0), jnp.moveaxis(carried...]
  transfers between devices with their start and end apart: 6 -> 11, of which waited for: 2 -> 1; matrix products, arithmetic and copies ran while one was open for 2% -> 11% of each run, Pallas kernels for 0% -> 10%
where the time goes in v1:
time: 404 us; the launch traced here: 396 us
  Pallas kernels  158 us (39%)
  blocking collectives  91 us (23%)
  waiting for transfers between devices  45.4 us (11%)
  matrix products  27.2 us (7%)
  starting transfers between devices  21.4 us (5%)
  local copies, waits for them, and re-layouts  20.5 us (5%)
  other arithmetic  16.3 us (4%)
  between operations  16.2 us (4%)
    pallas_call x1, Pallas kernels, body(): call(tail_kernel, (count, tiles), [tiled(), tiled(), tiled(), normed_spec...  71 us
    psum x1, waiting for transfers between devices, body(): lax.psum((jnp.sum(dtaps, axis=1), g_query, g_key, g_value, g_decay_down,...  45.3 us
    psum x1, blocking collectives, body(): lax.psum((jnp.sum(dtaps, axis=1), g_query, g_key, g_value, g_decay_down,...  39.2 us
    all_gather x1, blocking collectives, body(): lax.all_gather(jnp.concatenate([lax.psum(dmod, 'seq'), features, first, e...  30.9 us
    dot_general x13, matrix products, product(): return jnp.dot(left, right, precision=HIGH, preferred_element_type=F32)  27.2 us
    pallas_call x1, Pallas kernels, body(): call(front_kernel, (count,), [per_image(row), per_image((GRID, width)), p...  22.7 us
    pallas_call x1, Pallas kernels, body(): call(inner_back_kernel, (count, tiles), [tiled()] * 5 + [score_spec, pair...  18.4 us
    pallas_call x1, Pallas kernels, body(): call(state_back_kernel, (count, tiles), [turned()] * 10 + [pl.BlockSpec((...  15.9 us
  transfers between devices with their start and end apart: 11, of which 1 were waited for; matrix products, arithmetic and copies ran while one was open for 11% of the time, Pallas kernels for 10%

profile of v1, /device:TPU:0, one launch (start us, length us, event | category | flops | bytes accessed | tf_op | source)
XLA Modules:
  0.0 396.3 jit_solution(7040824473634157584)
XLA Ops:
  10.3 3.7 collective-permute-start
  28.9 3.0 pad_maximum_fusion.w_ref
  32.4 22.7 %shard_map.340 = (f32[1,1152,384]{2,1,0:T(8,128)}, f32[1,1024,384]{2,1,0:T(8,128)}, f32[1,1024,384]{2,1,0:T(8,128)}, f32[1,1024,384]{2,1,0:T(8,128)}, f32[1,1024...) custom-call(s32[2]{0:T(128)} %add_convert_fusion.edge_ref, ...), custom_call_target="tpu_custom_call" | custom-call | flops 3623878656 | bytes 15728640 | tf_op jit(solution)/shard_map/pallas_call | solution.py:834
  55.8 3.8 collective-permute-start.4
  63.2 12.8 %shard_map.341 = (f32[1,1024,384]{2,1,0:T(8,128)}, f32[1,8,3,256,128]{4,3,2,1,0:T(8,128)}, f32[1,1024,384]{2,1,0:T(8,128)}) custom-call(f32[1,1024,384]{2,1,0:T(8,128)} %get-tuple-element.52.q_ref, f32[1,1024,384]{2,1,0:T(8,128)} %get-tuple-element.53.k_ref, f32[1,1024,384]{2,1,0:T(8,128)} %get-tuple-element.54.v_ref, ...), custom_call_target="tpu_custom_call" | custom-call | flops 1811939328 | bytes 14155776 | tf_op jit(solution)/shard_map/pallas_call | solution.py:880
  76.8 71.0 %shard_map.342 = (f32[1,1024,384]{2,1,0:T(8,128)}, f32[1,1024,384]{2,1,0:T(8,128)}, f32[1,1024,384]{2,1,0:T(8,128)}, f32[1,1024,384]{2,1,0:T(8,128)}, f32[384,38...) custom-call(f32[1,1024,384]{2,1,0:T(8,128)} %get-tuple-element.58.o_, ...), custom_call_target="tpu_custom_call" | custom-call | flops 27179089920 | bytes 18874368 | tf_op jit(solution)/shard_map/pallas_call | solution.py:904
  152.9 18.4 %shard_map.343 = (f32[1,1024,384]{2,1,0:T(8,128)}, f32[1,1024,384]{2,1,0:T(8,128)}, f32[1,1024,384]{2,1,0:T(8,128)}, f32[1,8,3,128,128]{4,3,2,1,0:T(8,128)}) custom-call(f32[1,1024,384]{2,1,0:T(8,128)} %get-tuple-element.52.q_ref, f32[1,1024,384]{2,1,0:T(8,128)} %get-tuple-element.53.k_ref, f32[1,1024,384]{2,1,0:T(8,128)} %get-tuple-element.54.v_ref, ...), custom_call_target="tpu_custom_call" | custom-call | flops 1811939328 | bytes 18874368 | tf_op jit(solution)/shard_map/pallas_call | solution.py:948
  172.2 15.9 %shard_map.344 = (f32[1,1024,1536]{2,1,0:T(8,128)}, f32[1,1024,384]{2,1,0:T(8,128)}, f32[8,384]{1,0:T(8,128)}) custom-call(s32[1]{0:T(128)} %bitcast.2.real_ref, f32[1,1024,384]{2,1,0:T(8,128)} %get-tuple-element.52.q_ref, f32[1,1024,384]{2,1,0:T(8,128)} %get-tuple-element.53.k_ref, f32[1,1024,384]{2,1,0:T(8,128)} %get-tuple-element.54.v_ref, ...), custom_call_target="tpu_custom_call" | custom-call | flops 4529848320 | bytes 25165824 | tf_op jit(solution)/shard_map/pallas_call | solution.py:965
  188.1 9.1 %shard_map.346 = f32[384,1536]{1,0:T(8,128)} custom-call(f32[1,1024,384]{2,1,0:T(8,128)} %get-tuple-element.64.conv_ref, f32[1,1024,1536]{2,1,0:T(8,128)} %get-tuple-element.80.proj_ref), custom_call_target="tpu_custom_call" | custom-call | flops 3623878656 | bytes 11010048 | tf_op jit(solution)/shard_map/pallas_call | solution.py:1007
  197.2 2.7 fusion.35
  201.8 12.3 %all-reduce = s32[8]{0:T(128)} all-reduce(s32[8]{0:T(128)S(1)} %dynamic-update-slice), channel_id=1, replica_groups=mesh['img'=8,'seq'=4] {'img'}, use_global_device_ids=true, to_apply=%add | all-reduce | flops 8 | bytes 64
  217.1 3.7 collective-permute-start.8
  220.8 2.3 fusion.1
  223.1 2.1 convolution_bitcast_fusion
  225.8 8.6 %shard_map.345 = (f32[1,1024,384]{2,1,0:T(8,128)}, f32[1,8,384]{2,1,0:T(8,128)}, f32[9,8,384]{2,1,0:T(8,128)}) custom-call(f32[1,1024,384]{2,1,0:T(8,128)} %tok_ref.5, f32[1,1152,384]{2,1,0:T(8,128)} %get-tuple-element.57.normed_ref, f32[1,1024,384]{2,1,0:T(8,128)} %get-tuple-element.73.dconv_ref, f32[1,64,384]{2,1,0:T(8,128)} %collective-permute-done.8.top_ref, ...), custom_call_target="tpu_custom_call" | custom-call | flops 39321600 | bytes 9437184 | tf_op jit(solution)/shard_map/pallas_call | solution.py:1017
  237.3 8.5 %psum.84 = f32[1,2304]{1,0:T(1,128)S(1)} all-reduce(f32[1,2304]{1,0:T(1,128)} %bitcast.64), channel_id=1, replica_groups=mesh['img'=8,'seq'=4] {'seq'}, use_global_device_ids=true, to_apply=%region_1.2 | all-reduce | flops 2304 | bytes 18432 | tf_op jit(solution)/shard_map/psum | solution.py:1062
  246.6 30.9 %all-gather = f32[8,1,3328]{2,1,0:T(1,128)S(1)} all-gather(f32[1,1,3328]{2,1,0:T(1,128)S(1)} %bitcast.63), channel_id=1, replica_groups=mesh['img'=8,'seq'=4] {'img'}, dimensions={0}, use_global_device_ids=true | all-gather | bytes 119808 | tf_op jit(solution)/shard_map/all_gather | solution.py:1061
  278.2 39.2 %all-reduce.1 = (f32[9,384]{1,0:T(8,128)}, f32[384,16]{0,1:T(8,128)}, f32[16,384]{1,0:T(8,128)}, f32[384]{0:T(512)}) all-reduce(f32[9,384]{1,0:T(8,128)} %reduce_sum.41, f32[384,16]{0,1:T(8,128)} %fusion.1, f32[16,384]{1,0:T(8,128)} %convolution_bitcast_fusion, f32[384]{0:T(512)} %reduce_sum.42), channel_id=1, replica_groups=mesh['img'=8,'seq'=4] {'img','seq'}, use_global_device_ids=true, to_apply=%region_4.5 | all-reduce | flops 16128 | bytes 129024 | tf_op jit(solution)/shard_map/psum | solution.py:1047
  319.0 3.9 convolution_multiply_fusion
  326.4 2.1 fusion.3
  328.4 4.8 %fusion.13 = f32[384,2304]{1,0:T(8,128)} fusion(f32[8,3328]{1,0:T(8,128)S(1)} %bitcast.62), kind=kOutput, calls=%fused_computation.31 | convolution fusion | flops 84946944 | bytes 3624960 | tf_op jit(solution)/shard_map/dot_general | solution.py:30
  333.2 45.3 %all-reduce.5.cloned.1.call-done = (f32[384,384]{1,0:T(8,128)}, f32[384,384]{1,0:T(8,128)}, f32[384,384]{1,0:T(8,128)}, f32[384,384]{1,0:T(8,128)}, f32[384,384]...) async-done(((f32[384,384]{1,0:T(8,128)}, f32[384,384]{1,0:T(8,128)}, f32[384,384]{1,0:T(8,128)}, f32[384,384]{1,0:T(8,128)}, f32[384,384]{1,0:T(8,128)}, ...) | async-done | bytes 7667728 | tf_op jit(solution)/shard_map/psum | solution.py:1047
  378.5 2.0 copy.79
  380.6 2.1 copy.80
  (111 shorter events, 49.2 us)
Async XLA Ops:
  7.2 16.8 %copy-start = (f32[384,2304]{1,0:T(8,128)S(1)}, f32[384,2304]{1,0:T(8,128)}, u32[]{:S(2)}) copy-start(f32[384,2304]{1,0:T(8,128)} %param.28) | copy-start | bytes 10616836
  7.2 371.3 %all-reduce.5.cloned.1.call-start = ((), (), s32[]{:S(2)}) async-start(), calls=%async_computation | async-start | bytes 15335424 | tf_op jit(solution)/shard_map/psum | solution.py:1047
  9.0 23.4 %collective-permute-start.1 = (f32[1,64,384]{2,1,0:T(8,128)}, f32[1,64,384]{2,1,0:T(8,128)}, u32[]{:S(2)}, u32[]{:S(2)}) collective-permute-start(f32[1,64,384]{2,1,0:T(8,128)} %get-tuple-element.108), channel_id=1, source_target_pairs={{1,0},{2,1},{3,2},{5,4},{6,5},{7,6},{9,8},{10,9},{11,10},{13,12},{... | collective-permute-start | bytes 294920 | tf_op jit(solution)/shard_map/ppermute | solution.py:801
  10.3 22.1 %collective-permute-start = (f32[1,64,384]{2,1,0:T(8,128)}, f32[1,64,384]{2,1,0:T(8,128)}, u32[]{:S(2)}, u32[]{:S(2)}) collective-permute-start(f32[1,64,384]{2,1,0:T(8,128)} %get-tuple-element.109), channel_id=1, source_target_pairs={{0,1},{1,2},{2,3},{4,5},{5,6},{6,7},{8,9},{9,10},{10,11},{12,13},{... | collective-permute-start | bytes 294920 | tf_op jit(solution)/shard_map/ppermute | solution.py:800
  21.3 4.4 %copy-start.8 = (f32[2304]{0:T(1024)S(1)}, f32[2304]{0:T(1024)}, u32[]{:S(2)}) copy-start(f32[2304]{0:T(1024)} %param.29) | copy-start | bytes 27652
  55.8 20.1 %collective-permute-start.4 = (f32[1,3,72,128]{3,2,1,0:T(8,128)}, f32[1,3,72,128]{3,2,1,0:T(8,128)S(1)}, u32[]{:S(2)}, u32[]{:S(2)}) collective-permute-start(f32[1,3,72,128]{3,2,1,0:T(8,128)} %get-tuple-element.61), channel_id=1, source_target_pairs={{0,3},{4,7},{8,11},{12,15},{16,19},{20,23},{24,27},{28,31}} | collective-permute-start | bytes 331784 | tf_op jit(solution)/shard_map/ppermute | solution.py:760
  59.7 16.3 %collective-permute-start.3 = (f32[1,3,72,128]{3,2,1,0:T(8,128)}, f32[1,3,72,128]{3,2,1,0:T(8,128)S(1)}, u32[]{:S(2)}, u32[]{:S(2)}) collective-permute-start(f32[1,3,72,128]{3,2,1,0:T(8,128)} %get-tuple-element.61), channel_id=1, source_target_pairs={{0,2},{1,3},{4,6},{5,7},{8,10},{9,11},{12,14},{13,15},{16,18},{17,... | collective-permute-start | bytes 331784 | tf_op jit(solution)/shard_map/ppermute | solution.py:760
  61.4 14.6 %collective-permute-start.2 = (f32[1,3,72,128]{3,2,1,0:T(8,128)}, f32[1,3,72,128]{3,2,1,0:T(8,128)S(1)}, u32[]{:S(2)}, u32[]{:S(2)}) collective-permute-start(f32[1,3,72,128]{3,2,1,0:T(8,128)} %get-tuple-element.61), channel_id=1, source_target_pairs={{0,1},{1,2},{2,3},{4,5},{5,6},{6,7},{8,9},{9,10},{10,11},{12,13},{... | collective-permute-start | bytes 331784 | tf_op jit(solution)/shard_map/ppermute | solution.py:760
  148.8 22.5 %collective-permute-start.7 = (f32[1,3,72,128]{3,2,1,0:T(8,128)S(1)}, f32[1,3,72,128]{3,2,1,0:T(8,128)S(1)}, u32[]{:S(2)}, u32[]{:S(2)}) collective-permute-start(f32[1,3,72,128]{3,2,1,0:T(8,128)S(1)} %pad_maximum_fusion.3), channel_id=1, source_target_pairs={{3,0},{7,4},{11,8},{15,12},{19,16},{23,20},{27,24},{31,28}} | collective-permute-start | bytes 331784 | tf_op jit(solution)/shard_map/ppermute | solution.py:760
  150.1 21.3 %collective-permute-start.6 = (f32[1,3,72,128]{3,2,1,0:T(8,128)S(1)}, f32[1,3,72,128]{3,2,1,0:T(8,128)S(1)}, u32[]{:S(2)}, u32[]{:S(2)}) collective-permute-start(f32[1,3,72,128]{3,2,1,0:T(8,128)S(1)} %pad_maximum_fusion.3), channel_id=1, source_target_pairs={{2,0},{3,1},{6,4},{7,5},{10,8},{11,9},{14,12},{15,13},{18,16},{19,... | collective-permute-start | bytes 331784 | tf_op jit(solution)/shard_map/ppermute | solution.py:760
  151.4 20.0 %collective-permute-start.5 = (f32[1,3,72,128]{3,2,1,0:T(8,128)S(1)}, f32[1,3,72,128]{3,2,1,0:T(8,128)S(1)}, u32[]{:S(2)}, u32[]{:S(2)}) collective-permute-start(f32[1,3,72,128]{3,2,1,0:T(8,128)S(1)} %pad_maximum_fusion.3), channel_id=1, source_target_pairs={{1,0},{2,1},{3,2},{5,4},{6,5},{7,6},{9,8},{10,9},{11,10},{13,12},{... | collective-permute-start | bytes 331784 | tf_op jit(solution)/shard_map/ppermute | solution.py:760
  199.8 25.4 %copy-start.10 = (f32[8,384]{1,0:T(8,128)S(1)}, f32[8,384]{1,0:T(8,128)}, u32[]{:S(2)}) copy-start(f32[8,384]{1,0:T(8,128)} %get-tuple-element.81) | copy-start | bytes 36868
  215.8 10.1 %collective-permute-start.9 = (f32[1,64,384]{2,1,0:T(8,128)}, f32[1,64,384]{2,1,0:T(8,128)}, u32[]{:S(2)}, u32[]{:S(2)}) collective-permute-start(f32[1,64,384]{2,1,0:T(8,128)} %get-tuple-element.106), channel_id=1, source_target_pairs={{1,0},{2,1},{3,2},{5,4},{6,5},{7,6},{9,8},{10,9},{11,10},{13,12},{... | collective-permute-start | bytes 294920 | tf_op jit(solution)/shard_map/ppermute | solution.py:801
  217.1 8.8 %collective-permute-start.8 = (f32[1,64,384]{2,1,0:T(8,128)}, f32[1,64,384]{2,1,0:T(8,128)}, u32[]{:S(2)}, u32[]{:S(2)}) collective-permute-start(f32[1,64,384]{2,1,0:T(8,128)} %get-tuple-element.107), channel_id=1, source_target_pairs={{0,1},{1,2},{2,3},{4,5},{5,6},{6,7},{8,9},{9,10},{10,11},{12,13},{... | collective-permute-start | bytes 294920 | tf_op jit(solution)/shard_map/ppermute | solution.py:800
  225.8 8.6 %copy-start.9 = (f32[1,8,384]{2,1,0:T(8,128)S(1)}, f32[1,8,384]{2,1,0:T(8,128)}, u32[]{:S(2)}) copy-start(f32[1,8,384]{2,1,0:T(8,128)} %get-tuple-element.78) | copy-start | bytes 36868
  225.8 20.8 %copy-start.11 = (f32[384]{0:T(512)S(1)}, f32[384]{0:T(512)}, u32[]{:S(2)}) copy-start(f32[384]{0:T(512)} %get-tuple-element.102) | copy-start | bytes 4612
  317.4 5.5 %copy-start.3 = (f32[384,384]{1,0:T(8,128)S(1)}, f32[384,384]{1,0:T(8,128)}, u32[]{:S(2)}) copy-start(f32[384,384]{1,0:T(8,128)} %param.26) | copy-start | bytes 1769476
  317.4 5.5 %copy-start.4 = (f32[8,1,3328]{2,0,1:T(8,128)S(1)}, f32[8,1,3328]{2,0,1:T(8,128)}, u32[]{:S(2)}) copy-start(f32[8,1,3328]{2,0,1:T(8,128)} %copy.58) | copy-start | bytes 319492
  319.0 7.4 %copy-start.12 = (s32[8]{0:T(128)S(1)}, s32[8]{0:T(128)}, u32[]{:S(2)}) copy-start(s32[8]{0:T(128)} %all-reduce) | copy-start | bytes 100
  378.5 4.1 %copy-start.7 = (f32[384,384]{1,0:T(8,128)S(1)}, f32[384,384]{1,0:T(8,128)}, u32[]{:S(2)}) copy-start(f32[384,384]{1,0:T(8,128)} %get-tuple-element.124) | copy-start | bytes 1769476
  378.5 4.9 %copy-start.6 = (f32[384,384]{1,0:T(8,128)S(1)}, f32[384,384]{1,0:T(8,128)}, u32[]{:S(2)}) copy-start(f32[384,384]{1,0:T(8,128)} %get-tuple-element.128) | copy-start | bytes 1769476
  378.5 5.8 %copy-start.5 = (f32[384,384]{1,0:T(8,128)S(1)}, f32[384,384]{1,0:T(8,128)}, u32[]{:S(2)}) copy-start(f32[384,384]{1,0:T(8,128)} %get-tuple-element.129) | copy-start | bytes 1769476
  380.6 4.5 %copy-start.2 = (f32[384,1536]{1,0:T(8,128)S(1)}, f32[384,1536]{1,0:T(8,128)}, u32[]{:S(2)}) copy-start(f32[384,1536]{1,0:T(8,128)} %get-tuple-element.130) | copy-start | bytes 7077892
  385.1 2.5 copy-start.1
  (1 other events, 0.7 us)
Sparse Core Ops, SparseCore 0:
  200.0 178.5 all-reduce.4

commit v2 on v1

v2 whole, which is shorter than its diff:
```python
import functools
import math

import jax
import jax.numpy as jnp
from jax import lax
from jax.experimental import pallas as pl
from jax.experimental.pallas import tpu as pltpu
from jax.sharding import PartitionSpec as P

HEADS = 6
HEAD_DIM = 64
CLASSES = 1000
FREQ = 256
GRID = 64
WIDTH = 384
PAIRS = 3
LANES = 128
CHUNK = 128
TILE = 256
BLOCK = 768
ROWS = 1280
SMALL = 48
SPAN = 120.0
HIGH = lax.Precision.HIGHEST
F32 = jnp.float32
BF16 = jnp.bfloat16
GELU_C = math.sqrt(2.0 / math.pi)


def product(left, right):
    return jnp.dot(left, right, precision=HIGH, preferred_element_type=F32)


def dot(a, b, ca=1, cb=0):
    return lax.dot_general(a, b, (((ca,), (cb,)), ((), ())), preferred_element_type=F32)


def split(x):
    high = x.astype(BF16)
    return high, (x - high.astype(F32)).astype(BF16)


def mm3(a, b, ca=1, cb=0):
    return dot(a[0], b[0], ca, cb) + dot(a[1], b[0], ca, cb) + dot(a[0], b[1], ca, cb)


def split3(x):
    high = x.astype(BF16)
    rest = x - high.astype(F32)
    middle = rest.astype(BF16)
    return high, middle, (rest - middle.astype(F32)).astype(BF16)


def mm6(a, b, ca=1, cb=0):
    terms = ((0, 0), (0, 1), (1, 0), (1, 1), (0, 2), (2, 0))
    return sum(dot(a[i], b[j], ca, cb) for i, j in reversed(terms))


def wide6(x):
    h, m, l = split3(x)
    return jnp.concatenate([h, h, m, m, h, l], axis=1)


def tall6(w):
    h, m, l = split3(w)
    return jnp.concatenate([h, m, h, m, l, h], axis=0)


def wide3(x):
    high, low = split(x)
    return jnp.concatenate([high, high, low], axis=1)


def wide(x):
    high, low = split(x)
    return jnp.concatenate([high, low, high], axis=1)


def tall(w):
    high, low = split(w)
    return jnp.concatenate([high, high, low], axis=0)


def across(w):
    high, low = split(w)
    return jnp.concatenate([high, high, low], axis=1)


def lanes(x, p):
    return x[..., p * LANES : (p + 1) * LANES]


def first_half(shape):
    return lax.broadcasted_iota(jnp.int32, shape, len(shape) - 1) < HEAD_DIM


def block_diagonal(square):
    rows = lax.broadcasted_iota(jnp.int32, square.shape, 0) < HEAD_DIM
    return jnp.where(rows == first_half(square.shape), square, 0.0)


def head_mean(x):
    rows = lax.broadcasted_iota(jnp.int32, (LANES, LANES), 0) < HEAD_DIM
    ones = jnp.where(rows == first_half((LANES, LANES)), 1.0 / HEAD_DIM, 0.0).astype(BF16)
    high, low = split(x)
    return dot(
        jnp.concatenate([high, low], axis=1), jnp.concatenate([ones, ones], axis=0)
    )


def head_means(x):
    return jnp.concatenate([head_mean(lanes(x, p)) for p in range(PAIRS)], axis=1)


def stacked_heads(x):
    keep = first_half(x.shape)
    zero = jnp.zeros_like(x)
    return jnp.concatenate([jnp.where(keep, x, zero), jnp.where(keep, zero, x)], axis=0)


def merged_heads(x):
    rows = x.shape[0] // 2
    return jnp.where(first_half((rows, LANES)), x[:rows], x[rows:])


def sigmoid(x):
    return 1.0 / (1.0 + jnp.exp(-x))


def shifted(x, step):
    rows = x.shape[0]
    column = lax.broadcasted_iota(jnp.int32, x.shape, 0) % GRID
    if step == 1:
        return jnp.where(column == 0, 0.0, pltpu.roll(x, 1, 0))
    return jnp.where(column == GRID - 1, 0.0, pltpu.roll(x, rows - 1, 0))


def normalized(x):
    center = x - jnp.mean(x, axis=-1, keepdims=True)
    rate = lax.rsqrt(jnp.mean(center * center, axis=-1, keepdims=True) + 1e-06)
    return center * rate, rate


def normal_back(dhat, hat, rate):
    return rate * (
        dhat
        - jnp.mean(dhat, axis=-1, keepdims=True)
        - hat * jnp.mean(dhat * hat, axis=-1, keepdims=True)
    )


def triangle(size, upper):
    rows = lax.broadcasted_iota(jnp.int32, (size, size), 0)
    cols = lax.broadcasted_iota(jnp.int32, (size, size), 1)
    return jnp.where(cols >= rows if upper else cols <= rows, 1.0, 0.0).astype(BF16)


def running_sum(x, upper):
    tri = triangle(x.shape[0], upper)
    high = x.astype(BF16)
    rest = x - high.astype(F32)
    middle = rest.astype(BF16)
    low = (rest - middle.astype(F32)).astype(BF16)
    return dot(tri, high) + dot(tri, middle) + dot(tri, low)


def opening(tile):
    return (lax.axis_index("seq") == 0) & (tile == 0)


def spread(compact):
    keep = first_half(compact.shape)
    return jnp.concatenate(
        [jnp.where(keep, compact, 0.0), jnp.where(keep, 0.0, compact)], axis=0
    )


def linked(parts, p):
    total = jnp.zeros((HEAD_DIM, LANES), F32)
    for part in reversed(parts):
        total = part[p, 0:HEAD_DIM, :] + part[p, HEAD_DIM : HEAD_DIM + 1, :] * total
    return spread(total)


def as_column(row):
    return jnp.broadcast_to(row, (8, row.shape[1])).T[:, 0:1]


def applied(row, w_ref):
    return jnp.sum(as_column(row) * w_ref[...], axis=0, keepdims=True)


def condition_kernel(ids_ref, feat_ref, first_w_ref, second_w_ref, row_ref, ada_ref, bias_ref, mod_ref, info_ref):
    features = feat_ref[...]
    first = applied(features, first_w_ref)
    embed = applied(first * sigmoid(first), second_w_ref)
    at = lax.broadcasted_iota(jnp.int32, row_ref.shape, 0) == ids_ref[pl.program_id(0)] % 8
    embed = embed + jnp.sum(jnp.where(at, row_ref[...], 0.0), axis=0, keepdims=True)
    modul = applied(embed * sigmoid(embed), ada_ref)
    for j in range(6):
        at = slice(j * WIDTH, (j + 1) * WIDTH)
        mod_ref[j : j + 1, :] = modul[:, at] + bias_ref[at][None, :]
    info_ref[...] = jnp.zeros_like(info_ref)
    info_ref[0:1, 0:FREQ] = features
    info_ref[1:2, :] = first
    info_ref[2:3, :] = embed


def embed_kernel(ids_ref, rows_ref, ada_ref, second_ref, gf_ref, gs_ref, gc_ref, ga_ref, gb_ref):
    images = rows_ref.shape[1]
    features, first, embed = rows_ref[6][:, 0:FREQ], rows_ref[7], rows_ref[8]

    def silu_back(x, grad):
        sig = sigmoid(x)
        return grad * (sig * (1.0 + x * (1.0 - sig)))

    act = split((embed * sigmoid(embed)).T)
    dembed = jnp.zeros((images, WIDTH), F32)
    for j in range(6):
        at = slice(j * WIDTH, (j + 1) * WIDTH)
        dmod = split(rows_ref[j])
        ga_ref[:, at] = mm3(act, dmod)
        gb_ref[:, at] = jnp.sum(rows_ref[j], axis=0, keepdims=True)
        dembed = dembed + mm3(dmod, split(ada_ref[:, at]), 1, 1)
    dembed = silu_back(embed, dembed)
    gc_ref[...] = jnp.zeros_like(gc_ref)

    def put(n, carry):
        mine = lax.broadcasted_iota(jnp.int32, (images, WIDTH), 0) == n
        row = jnp.sum(jnp.where(mine, dembed, 0.0), axis=0, keepdims=True)
        gc_ref[pl.ds(ids_ref[n], 1), :] += row
        return carry

    lax.fori_loop(0, images, put, 0)
    de = split(dembed)
    gs_ref[...] = mm3(split((first * sigmoid(first)).T), de)
    dfirst = silu_back(first, mm3(de, split(second_ref[...]), 1, 1))
    gf_ref[...] = mm3(split(features.T), split(dfirst))


def front_kernel(
    tok_ref,
    top_ref,
    bot_ref,
    valid_ref,
    mod_ref,
    taps_ref,
    wq_ref,
    wk_ref,
    wv_ref,
    down_ref,
    up_ref,
    bias_ref,
    w_ref,
    normed_ref,
    conv_ref,
    q_ref,
    k_ref,
    v_ref,
    cum_ref,
    slope_ref,
    far_ref,
    state_ref,
    fade_ref,
    out_ref,
    w3_ref,
    proj_ref,
    st_ref,
    dev_ref,
):
    image, i = pl.program_id(0), pl.program_id(1)
    length = tok_ref.shape[0]

    @pl.when((image == 0) & (i == 0))
    def _():
        w_ref[:, 0:WIDTH] = wq_ref[...] * HEAD_DIM ** (-0.5)
        w_ref[:, WIDTH : 2 * WIDTH] = wk_ref[...]
        w_ref[:, 2 * WIDTH : 3 * WIDTH] = wv_ref[...]
        w_ref[:, 3 * WIDTH :] = mm6(split3(down_ref[...]), split3(up_ref[...]), 0, 0)
        w3_ref[...] = tall6(w_ref[...])

    real = jnp.sum(valid_ref[...], axis=1, keepdims=True)
    shift = mod_ref[0:1, :]
    scale = 1.0 + mod_ref[1:2, :]

    def modulated(x):
        return normalized(x)[0] * scale + shift

    @pl.when(i == 0)
    def _():
        normed_ref[0:GRID, :] = jnp.where(
            lax.axis_index("seq") == 0, 0.0, modulated(top_ref[...])
        )
        normed_ref[pl.ds(length + GRID, GRID), :] = jnp.where(
            lax.axis_index("seq") == lax.axis_size("seq") - 1, 0.0, modulated(bot_ref[...])
        )
        for at in range(0, length, TILE):
            normed_ref[GRID + at : GRID + at + TILE, :] = modulated(tok_ref[at : at + TILE, :])
        st_ref[...] = jnp.zeros_like(st_ref)
        dev_ref[...] = jnp.zeros_like(dev_ref)

    start = pl.multiple_of(i * TILE, TILE)
    rows = [normed_ref[pl.ds(start + a * GRID, TILE), :] for a in range(3)]
    parts = [
        sum(taps_ref[3 * a + b : 3 * a + b + 1, :] * rows[a] for a in range(3))
        for b in range(3)
    ]
    conv = shifted(parts[0], 1) + parts[1] + shifted(parts[2], -1)
    conv_ref[...] = conv
    hidden = conv * sigmoid(conv)
    first = opening(i)

    @pl.when(first)
    def _():
        proj_ref[...] = dot(wide6(hidden), w3_ref[...])

    @pl.when(jnp.logical_not(first))
    def _():
        proj_ref[...] = dot(wide3(hidden), w3_ref[0 : 3 * WIDTH, :])

    proj = proj_ref[...]
    keep = (
        lax.broadcasted_iota(jnp.int32, (TILE, WIDTH), 0) + start < real
    )
    q = proj[:, :WIDTH]
    k = jnp.where(keep, proj[:, WIDTH : 2 * WIDTH], 0.0)
    v = jnp.where(keep, proj[:, 2 * WIDTH : 3 * WIDTH], 0.0)
    x = proj[:, 3 * WIDTH :] + bias_ref[...][None, :]
    small = jnp.exp(-jnp.abs(x))
    gates = jnp.where(keep, (jnp.minimum(x, 0.0) - jnp.log1p(small)) * (1.0 / 16.0), 0.0)
    slope = jnp.where(x >= 0, small, 1.0) / (1.0 + small)
    slope_ref[...] = jnp.where(keep, slope * (1.0 / 16.0), 0.0)
    q_ref[...] = q
    k_ref[...] = k
    v_ref[...] = v
    for c in range(TILE // CHUNK):
        at = slice(c * CHUNK, (c + 1) * CHUNK)
        cum = running_sum(gates[at], False)
        cum_ref[at, :] = cum
        final = cum[CHUNK - 1 : CHUNK, :]
        dev = dev_ref[0:1, :]
        far_ref[at, :] = q[at] * jnp.exp(cum + dev)
        fade_ref[c] = jnp.broadcast_to(jnp.exp(dev), (8, WIDTH))
        kd = k[at] * jnp.exp(final - cum)
        factor = jnp.exp(final)
        for p in range(PAIRS):
            state_ref[c, p] = st_ref[p]
            update = mm3(split(lanes(v[at], p)), split(lanes(kd, p)), 0, 0)
            st_ref[p] = lanes(factor, p) * st_ref[p] + block_diagonal(update)
        dev_ref[...] = dev_ref[...] + final

    @pl.when(i == pl.num_programs(1) - 1)
    def _():
        for p in range(PAIRS):
            out_ref[p, 0:HEAD_DIM, :] = st_ref[p, 0:HEAD_DIM, :] + st_ref[p, HEAD_DIM:, :]
            out_ref[p, HEAD_DIM:, :] = jnp.exp(lanes(dev_ref[...], p))


def exact_scores(q_ref, k_ref, cum_ref, base, s_ref):
    q = q_ref[pl.ds(base, CHUNK), :]
    cum = cum_ref[pl.ds(base, CHUNK), :]
    s_ref[...] = jnp.zeros_like(s_ref)

    def step(j, carry):
        key = k_ref[pl.ds(base + j, 1), :]
        weight = jnp.exp(jnp.minimum(cum - cum_ref[pl.ds(base + j, 1), :], 0.0))
        terms = q * key * weight
        for p in range(PAIRS):
            column = jnp.sum(stacked_heads(lanes(terms, p)), axis=1, keepdims=True)
            at = lax.broadcasted_iota(jnp.int32, (2 * CHUNK, CHUNK), 1) == j
            s_ref[p] = jnp.where(at, column, s_ref[p])
        return carry

    lax.fori_loop(0, CHUNK, step, 0)


def causal_two():
    rows = lax.broadcasted_iota(jnp.int32, (2 * CHUNK, CHUNK), 0) % CHUNK
    return rows >= lax.broadcasted_iota(jnp.int32, (2 * CHUNK, CHUNK), 1)


def inner_kernel(
    q_ref, k_ref, v_ref, cum_ref, state_ref, normed_ref, gate_ref, o_ref, s_ref, gp_ref, w3_ref, tmp_ref
):
    @pl.when((pl.program_id(0) == 0) & (pl.program_id(1) == 0))
    def _():
        w3_ref[...] = tall(gate_ref[...])

    start = pl.multiple_of(pl.program_id(1) * TILE + GRID, GRID)
    gp_ref[...] = dot(wide(normed_ref[pl.ds(start, TILE), :]), w3_ref[...])
    mask = causal_two()
    for c in range(TILE // CHUNK):
        base = c * CHUNK
        at = slice(base, base + CHUNK)
        q = q_ref[at, :]
        k = k_ref[at, :]
        cum = cum_ref[at, :]
        final = cum[CHUNK - 1 : CHUNK, :]
        wild = jnp.max(-final) > SPAN
        middle = 0.5 * final
        qf = split3(q * jnp.exp(cum - middle))
        kf = split3(k * jnp.exp(middle - cum))
        for p in range(PAIRS):
            qp = tuple(stacked_heads(lanes(part, p)) for part in qf[:2])
            kp = tuple(lanes(part, p) for part in kf[:2])
            tmp_ref[p] = mm3(qp, kp, 1, 1)

        @pl.when(opening(pl.program_id(1)) & (c == 0))
        def _():
            for p in range(PAIRS):
                qp = tuple(stacked_heads(lanes(part, p)) for part in qf)
                kp = tuple(lanes(part, p) for part in kf)
                tmp_ref[p] = mm6(qp, kp, 1, 1)

        @pl.when(wild)
        def _():
            exact_scores(q_ref, k_ref, cum_ref, base, tmp_ref)

        qd = q * jnp.exp(cum)
        for p in range(PAIRS):
            s = jnp.where(mask, tmp_ref[p], 0.0)
            s_ref[c, p] = s
            inner = merged_heads(mm3(split(s), split(lanes(v_ref[at, :], p))))
            outer = mm3(split(lanes(qd, p)), split(state_ref[c, p]), 1, 1)
            o_ref[at, p * LANES : (p + 1) * LANES] = inner + outer


def mix_kernel(o_ref, far_ref, tok_ref, gp_ref, mod_ref, out_w_ref, *rest):
    parts, (mid_ref, branch_ref, att_ref, st_ref, o3_ref) = rest[:-5], rest[-5:]
    image, tile = pl.program_id(0), pl.program_id(1)

    @pl.when((image == 0) & (tile == 0))
    def _():
        o3_ref[...] = tall(out_w_ref[...])

    @pl.when(tile == 0)
    def _():
        for p in range(PAIRS):
            st_ref[p] = linked(parts, p)

    far = split(far_ref[...])
    att = o_ref[...] + jnp.concatenate(
        [
            mm3(tuple(lanes(part, p) for part in far), split(st_ref[p]), 1, 1)
            for p in range(PAIRS)
        ],
        axis=1,
    )
    att_ref[...] = att
    rate = lax.rsqrt(head_means(att * att) + 1e-05)
    gp = gp_ref[...]
    branch = dot(wide(att * rate * (gp * sigmoid(gp))), o3_ref[...])
    branch_ref[...] = branch
    mid_ref[...] = tok_ref[...] + mod_ref[2:3, :] * branch


def mlp_kernel(last, mid_ref, cot_ref, mod_ref, up_ref, down_ref, *rest):
    if last:
        mlp_in_ref, dsec_in_ref, block_ref, dmid_ref, dmod_ref = rest[:5]
    else:
        block_ref, dmid_ref = rest[:2]
    g_ref, u3_ref, ut_ref, d_ref, dt3_ref, gu_ref, gd_ref = rest[-7:]
    image, tile = pl.program_id(0), pl.program_id(1)

    @pl.when((image == 0) & (tile == 0))
    def _():
        u3_ref[...] = tall(up_ref[...])
        ut_ref[...] = jnp.concatenate(split(up_ref[...]), axis=0)
        d_ref[...] = jnp.concatenate(split(down_ref[...]), axis=0)
        dt3_ref[...] = across(down_ref[...])
        gu_ref[...] = jnp.zeros_like(gu_ref)
        gd_ref[...] = jnp.zeros_like(gd_ref)

    shift_b = mod_ref[3:4, :]
    scale_b = 1.0 + mod_ref[4:5, :]
    gate_b = mod_ref[5:6, :]
    middle = mid_ref[...]
    hat, rate_b = normalized(middle)
    second = hat * scale_b + shift_b
    cot = cot_ref[...]
    dmlp = cot * gate_b
    u = dot(wide(second), u3_ref[...])
    square = u * u
    th = jnp.tanh(GELU_C * (u + 0.044715 * u * square))
    slope = 0.5 * (1.0 + th) + 0.5 * u * (1.0 - th * th) * (
        GELU_C * (1.0 + 3.0 * 0.044715 * square)
    )
    act = split(0.5 * u * (1.0 + th))
    mlp = mm3(act, (d_ref[0:BLOCK, :], d_ref[BLOCK:, :]))
    du = split(dot(wide(dmlp), dt3_ref[...], 1, 1) * slope)
    dsec = mm3(du, (ut_ref[0:WIDTH, :], ut_ref[WIDTH:, :]), 1, 1)
    gu_ref[...] += mm3(split(second.T), du)
    gd_ref[...] += mm3(split(dmlp.T), act)
    if not last:
        block_ref[...] = mlp
        dmid_ref[...] = dsec
    else:
        mlp = mlp + mlp_in_ref[...]
        dsec = dsec + dsec_in_ref[...]
        block_ref[...] = middle + gate_b * mlp
        dmid_ref[...] = cot + normal_back(dsec * scale_b, hat, rate_b)

        @pl.when(tile == 0)
        def _():
            dmod_ref[...] = jnp.zeros_like(dmod_ref)

        dmod_ref[3:4, :] += jnp.sum(dsec, axis=0, keepdims=True)
        dmod_ref[4:5, :] += jnp.sum(dsec * hat, axis=0, keepdims=True)
        dmod_ref[5:6, :] += jnp.sum(cot * mlp, axis=0, keepdims=True)

    @pl.when((image == pl.num_programs(0) - 1) & (tile == pl.num_programs(1) - 1))
    def _():
        for j in range(BLOCK // WIDTH):
            at = slice(j * WIDTH, (j + 1) * WIDTH)
            g_ref[at, :] = gu_ref[:, at]
        g_ref[BLOCK:, :] = gd_ref[...].T


def mix_back_kernel(
    dmid_ref,
    branch_ref,
    att_ref,
    gp_ref,
    far_ref,
    normed_ref,
    mod_ref,
    message_ref,
    out_w_ref,
    gate_w_ref,
    datt_ref,
    dnorm_ref,
    g_ref,
    dmod_ref,
    dmessage_ref,
    ot3_ref,
    gt3_ref,
    dst_ref,
):
    image, tile = pl.program_id(0), pl.program_id(1)

    @pl.when((image == 0) & (tile == 0))
    def _():
        ot3_ref[...] = across(out_w_ref[...])
        gt3_ref[...] = across(gate_w_ref[...])
        g_ref[...] = jnp.zeros_like(g_ref)

    @pl.when(tile == 0)
    def _():
        dmod_ref[...] = jnp.zeros_like(dmod_ref)
        dst_ref[...] = jnp.zeros_like(dst_ref)

    dmid = dmid_ref[...]
    dmod_ref[2:3, :] += jnp.sum(dmid * branch_ref[...], axis=0, keepdims=True)
    dbr = split(dmid * mod_ref[2:3, :])
    dy = dot(jnp.concatenate([dbr[0], dbr[1], dbr[0]], axis=1), ot3_ref[...], 1, 1)
    att = att_ref[...]
    rate = lax.rsqrt(head_means(att * att) + 1e-05)
    unit = att * rate
    gp = gp_ref[...]
    sig = sigmoid(gp)
    gate = gp * sig
    g_ref[0:WIDTH, :] += mm3(split(unit * gate), dbr, 0, 0)
    dunit = dy * gate
    datt = rate * (dunit - unit * head_means(dunit * unit))
    datt_ref[...] = datt
    dg = split((dy * unit) * (sig * (1.0 + gp * (1.0 - sig))))
    dnorm_ref[...] = dot(jnp.concatenate([dg[0], dg[1], dg[0]], axis=1), gt3_ref[...], 1, 1)
    start = pl.multiple_of(tile * TILE + GRID, GRID)
    g_ref[WIDTH:, :] += mm3(split(normed_ref[pl.ds(start, TILE), :]), dg, 0, 0)
    da = split(datt)
    far = split(far_ref[...])
    for p in range(PAIRS):
        dst_ref[p] += block_diagonal(
            mm3(tuple(lanes(part, p) for part in da), tuple(lanes(part, p) for part in far), 0, 0)
        )

    @pl.when(tile == pl.num_programs(1) - 1)
    def _():
        for p in range(PAIRS):
            dmessage_ref[p, 0:HEAD_DIM, :] = dst_ref[p, 0:HEAD_DIM, :] + dst_ref[p, HEAD_DIM:, :]
            dmessage_ref[p, HEAD_DIM:, :] = message_ref[p, HEAD_DIM:, :]


def exact_back(q_ref, k_ref, cum_ref, ds_ref, base, dq_ref, dk_ref):
    q = q_ref[pl.ds(base, CHUNK), :]
    cum = cum_ref[pl.ds(base, CHUNK), :]
    dq_ref[...] = jnp.zeros_like(dq_ref)

    def step(j, carry):
        key = k_ref[pl.ds(base + j, 1), :]
        weight = jnp.exp(jnp.minimum(cum - cum_ref[pl.ds(base + j, 1), :], 0.0))
        at = lax.broadcasted_iota(jnp.int32, (2 * CHUNK, CHUNK), 1) == j
        columns = []
        for p in range(PAIRS):
            column = jnp.sum(jnp.where(at, ds_ref[p], 0.0), axis=1, keepdims=True)
            columns.append(merged_heads(jnp.broadcast_to(column, (2 * CHUNK, LANES))))
        ds = jnp.concatenate(columns, axis=1) * weight
        dq_ref[...] += ds * key
        dk_ref[pl.ds(j, 1), :] = jnp.sum(ds * q, axis=0, keepdims=True)
        return carry

    lax.fori_loop(0, CHUNK, step, 0)


def inner_back_kernel(
    q_ref,
    k_ref,
    v_ref,
    cum_ref,
    datt_ref,
    s_ref,
    state_ref,
    fade_ref,
    st_ref,
    dq_ref,
    dk_ref,
    dv_ref,
    full_ref,
    ds_ref,
    dqi_ref,
    dki_ref,
):
    mask = causal_two()
    for c in range(TILE // CHUNK):
        base = c * CHUNK
        at = slice(base, base + CHUNK)
        q = q_ref[at, :]
        k = k_ref[at, :]
        cum = cum_ref[at, :]
        final = cum[CHUNK - 1 : CHUNK, :]
        wild = jnp.max(-final) > SPAN
        middle = 0.5 * final
        eq = jnp.exp(cum - middle)
        ek = jnp.exp(middle - cum)
        qf = split(q * eq)
        kf = split(k * ek)
        da = split3(datt_ref[at, :])
        vs = split3(v_ref[at, :])
        for p in range(PAIRS):
            da2 = tuple(stacked_heads(lanes(part, p)) for part in da[:2])
            vp = tuple(lanes(part, p) for part in vs[:2])
            ds_ref[p] = jnp.where(mask, mm3(da2, vp, 1, 1), 0.0)

        @pl.when(opening(pl.program_id(1)) & (c == 0))
        def _():
            for p in range(PAIRS):
                da2 = tuple(stacked_heads(lanes(part, p)) for part in da)
                vp = tuple(lanes(part, p) for part in vs)
                ds_ref[p] = jnp.where(mask, mm6(da2, vp, 1, 1), 0.0)

        for p in range(PAIRS):
            da2 = tuple(stacked_heads(lanes(part, p)) for part in da[:2])
            ds2 = split(ds_ref[p])
            kp = tuple(lanes(part, p) for part in kf)
            qp = tuple(lanes(part, p) for part in qf)
            dqi_ref[:, p * LANES : (p + 1) * LANES] = merged_heads(mm3(ds2, kp)) * lanes(eq, p)
            q2 = tuple(stacked_heads(part) for part in qp)
            dki_ref[:, p * LANES : (p + 1) * LANES] = mm3(ds2, q2, 0, 0) * lanes(ek, p)
            s2 = split(s_ref[c, p])
            dv_ref[at, p * LANES : (p + 1) * LANES] = mm3(s2, da2, 0, 0)

        @pl.when(wild)
        def _():
            exact_back(q_ref, k_ref, cum_ref, ds_ref, base, dqi_ref, dki_ref)

        grow = jnp.exp(cum)
        for p in range(PAIRS):
            full = state_ref[c, p] + lanes(fade_ref[c, 0:1, :], p) * st_ref[p]
            full_ref[c, p] = full
            outer = mm3(tuple(lanes(part, p) for part in da[:2]), split(full))
            dq_ref[at, p * LANES : (p + 1) * LANES] = (
                dqi_ref[:, p * LANES : (p + 1) * LANES] + outer * lanes(grow, p)
            )
        dk_ref[at, :] = dki_ref[...]


def state_back_kernel(
    valid_ref,
    q_ref,
    k_ref,
    v_ref,
    cum_ref,
    slope_ref,
    conv_ref,
    datt_ref,
    dq_ref,
    dk_ref,
    dv_ref,
    full_ref,
    w_ref,
    *rest,
):
    parts, (proj_ref, dconv_ref, dbias_ref, wt3_ref, dst_ref) = rest[:-5], rest[-5:]
    image, turn = pl.program_id(0), pl.program_id(1)
    tile = pl.num_programs(1) - 1 - turn

    @pl.when((image == 0) & (turn == 0))
    def _():
        wt3_ref[...] = across(w_ref[...])
        dbias_ref[...] = jnp.zeros_like(dbias_ref)

    @pl.when(turn == 0)
    def _():
        for p in range(PAIRS):
            dst_ref[p] = linked(parts, p)

    count = jnp.sum(valid_ref[...], axis=1, keepdims=True)
    keep = (
        lax.broadcasted_iota(jnp.int32, (CHUNK, WIDTH), 0) + tile * TILE
    )
    for c in reversed(range(TILE // CHUNK)):
        at = slice(c * CHUNK, (c + 1) * CHUNK)
        q = q_ref[at, :]
        k = k_ref[at, :]
        cum = cum_ref[at, :]
        final = cum[CHUNK - 1 : CHUNK, :]
        late = jnp.exp(final - cum)
        kd = k * late
        v = v_ref[at, :]
        qd = split(q * jnp.exp(cum))
        da = split(datt_ref[at, :])
        factor = jnp.exp(final)
        dk_parts, dv_parts, cross = [], [], []
        for p in range(PAIRS):
            old = dst_ref[p]
            pair = split(old)
            dk_parts.append(mm3(split(lanes(v, p)), pair))
            dv_parts.append(mm3(split(lanes(kd, p)), pair, 1, 1))
            leaving = lanes(factor, p) * full_ref[c, p] + block_diagonal(
                mm3(split(lanes(v, p)), split(lanes(kd, p)), 0, 0)
            )
            cross.append(jnp.sum(leaving * old, axis=0, keepdims=True))
            update = mm3(
                tuple(lanes(part, p) for part in da), tuple(lanes(part, p) for part in qd), 0, 0
            )
            dst_ref[p] = lanes(factor, p) * old + block_diagonal(update)
        dq = dq_ref[at, :]
        dk = dk_ref[at, :] + jnp.concatenate(dk_parts, axis=1) * late
        dv = dv_ref[at, :] + jnp.concatenate(dv_parts, axis=1)
        dgates = running_sum(q * dq - k * dk, True) + jnp.concatenate(cross, axis=1)
        dx = dgates * slope_ref[at, :]
        real = keep + c * CHUNK < count
        dk = jnp.where(real, dk, 0.0)
        dv = jnp.where(real, dv, 0.0)
        dbias_ref[...] += jnp.sum(dx.reshape(CHUNK // 8, 8, WIDTH), axis=0)
        proj_ref[at, 0:WIDTH] = dq
        proj_ref[at, WIDTH : 2 * WIDTH] = dk
        proj_ref[at, 2 * WIDTH : 3 * WIDTH] = dv
        proj_ref[at, 3 * WIDTH :] = dx
    dhidden = dot(wide(proj_ref[...]), wt3_ref[...], 1, 1)
    conv = conv_ref[...]
    sig = sigmoid(conv)
    dconv_ref[...] = dhidden * (sig * (1.0 + conv * (1.0 - sig)))


def weight_kernel(conv_ref, proj_ref, dbias_ref, down_ref, up_ref, g_ref, acc_ref):
    image, tile = pl.program_id(0), pl.program_id(1)

    @pl.when((image == 0) & (tile == 0))
    def _():
        acc_ref[...] = jnp.zeros_like(acc_ref)

    conv = conv_ref[...]
    hidden = split((conv * sigmoid(conv)).T)
    for j in range(4):
        at = slice(j * WIDTH, (j + 1) * WIDTH)
        acc_ref[:, at] += mm3(hidden, split(proj_ref[:, at]))

    @pl.when((image == pl.num_programs(0) - 1) & (tile == pl.num_programs(1) - 1))
    def _():
        for j in range(3):
            grad = acc_ref[:, j * WIDTH : (j + 1) * WIDTH]
            g_ref[j * WIDTH : (j + 1) * WIDTH, :] = (
                grad * HEAD_DIM ** (-0.5) if j == 0 else grad
            )
        grad = acc_ref[:, 3 * WIDTH :]
        base = 3 * WIDTH
        rank = up_ref.shape[0]
        g_ref[base:, :] = jnp.zeros_like(g_ref[base:, :])
        g_ref[base : base + rank, :] = mm6(split3(up_ref[...]), split3(grad), 1, 1)
        g_ref[base + rank : base + 2 * rank, :] = mm6(split3(down_ref[...]), split3(grad))
        g_ref[base + 2 * rank : base + 2 * rank + 1, :] = jnp.sum(
            dbias_ref[...], axis=0, keepdims=True
        )


def front_back_kernel(
    tok_ref,
    normed_ref,
    dconv_ref,
    top_ref,
    bot_ref,
    dnorm_ref,
    dmid_ref,
    mod_ref,
    taps_ref,
    grad_ref,
    dmod_ref,
    dtaps_ref,
    pad_ref,
    taps_acc_ref,
):
    length = dconv_ref.shape[0]
    image, i = pl.program_id(0), pl.program_id(1)

    @pl.when((image == 0) & (i == 0))
    def _():
        taps_acc_ref[...] = jnp.zeros_like(taps_acc_ref)

    @pl.when(i == 0)
    def _():
        dmod_ref[...] = jnp.zeros_like(dmod_ref)
        pad_ref[0:GRID, :] = top_ref[...]
        pad_ref[pl.ds(length + GRID, GRID), :] = bot_ref[...]
        pad_ref[pl.ds(GRID, length), :] = dconv_ref[...]

    scale = 1.0 + mod_ref[1:2, :]

    def eights(x):
        return jnp.sum(x.reshape(x.shape[0] // 8, 8, WIDTH), axis=0)

    start = pl.multiple_of(i * TILE, TILE)
    rows = [pad_ref[pl.ds(start + (2 - a) * GRID, TILE), :] for a in range(3)]
    parts = [
        sum(taps_ref[3 * a + b : 3 * a + b + 1, :] * rows[a] for a in range(3))
        for b in range(3)
    ]
    dn = (
        shifted(parts[0], -1)
        + parts[1]
        + shifted(parts[2], 1)
        + dnorm_ref[...]
    )
    hat, rate = normalized(tok_ref[...])
    grad_ref[...] = dmid_ref[...] + normal_back(
        dn * scale, hat, rate
    )
    dmod_ref[0:1, :] += jnp.sum(dn, axis=0, keepdims=True)
    dmod_ref[1:2, :] += jnp.sum(dn * hat, axis=0, keepdims=True)
    own = rows[1]
    moved = [shifted(own, -1), own, shifted(own, 1)]
    for a in range(3):
        near = normed_ref[pl.ds(start + a * GRID, TILE), :]
        for b in range(3):
            taps_acc_ref[3 * a + b] += eights(moved[b] * near)

    @pl.when((image == pl.num_programs(0) - 1) & (i == pl.num_programs(1) - 1))
    def _():
        dtaps_ref[...] = jnp.zeros_like(dtaps_ref)
        for t in range(9):
            dtaps_ref[t : t + 1, :] = jnp.sum(taps_acc_ref[t], axis=0, keepdims=True)


def call(kernel, grid, ins, outs, scratch, flops=0, moved=0, prefetch=0, limit=60):
    return pl.pallas_call(
        kernel,
        grid_spec=pltpu.PrefetchScalarGridSpec(
            num_scalar_prefetch=prefetch,
            grid=grid,
            in_specs=ins,
            out_specs=[spec for spec, _ in outs],
            scratch_shapes=scratch,
        ),
        out_shape=[jax.ShapeDtypeStruct(shape, F32) for _, shape in outs],
        compiler_params=pltpu.CompilerParams(vmem_limit_bytes=limit * 1024 * 1024),
        cost_estimate=pl.CostEstimate(flops=1, bytes_accessed=1, transcendentals=0),
    )


def whole(shape):
    zeros = (0,) * len(shape)
    return pl.BlockSpec(shape, lambda *_: zeros, pipeline_mode=pl.Buffered(1))


def per_image(shape):
    zeros = (0,) * len(shape)
    return pl.BlockSpec((None,) + shape, lambda n, *_: (n,) + zeros)


def time_features(timesteps):
    half = FREQ // 2
    freqs = jnp.exp(-math.log(10000.0) * jnp.arange(half, dtype=F32) / half)
    angles = timesteps.astype(F32)[:, None] * freqs[None, :]
    return jnp.concatenate([jnp.cos(angles), jnp.sin(angles)], axis=1)


def halves(axis):
    return [1 << b for b in range(lax.axis_size(axis).bit_length() - 1)]


def swapped(x, axis, bit):
    return lax.ppermute(x, axis, [(i, i ^ bit) for i in range(lax.axis_size(axis))])


def is_high(axis, bit):
    return (lax.axis_index(axis) // bit) % 2


def fold_kernel(links, *refs):
    ins, outs = refs[: 2 * len(links)], list(refs[2 * len(links) :])
    for n, link in enumerate(links):
        keep, got = ins[2 * n], ins[2 * n + 1]
        if link is None:
            outs.pop(0)[...] = keep[...] + got[...]
            continue
        half = keep.shape[0] // 2
        high = is_high(*link)
        for side in (1 - high, high):
            start = side * half
            at = pl.ds(pl.multiple_of(start, 8) if half % 8 == 0 else start, half)
            outs.pop(0)[...] = keep[at, :] + got[at, :]


def fold(flows):
    links = [flow.order[0] if flow.order else None for flow in flows]
    if any(flow.keep.shape[0] % 16 and flow.order for flow in flows):
        for flow, link in zip(flows, links):
            total = flow.keep + flow.got
            if link is None:
                flow.keep = total
            else:
                flow.halve(total)
        return
    shapes = []
    for flow, link in zip(flows, links):
        rows = flow.keep.shape[0]
        shapes += [(rows, WIDTH)] if link is None else [(rows // 2, WIDTH)] * 2
    outs = call(
        functools.partial(fold_kernel, links),
        (1,),
        [whole(x.shape) for flow in flows for x in (flow.keep, flow.got)],
        [(whole(shape), shape) for shape in shapes],
        [],
        limit=32,
    )(*(x for flow in flows for x in (flow.keep, flow.got)))
    outs = list(outs)
    for flow, link in zip(flows, links):
        if link is None:
            flow.keep = outs.pop(0)
        else:
            flow.sent, flow.keep = outs.pop(0), outs.pop(0)


class Flow:
    def __init__(self, x, order):
        self.order, self.used = list(order), []
        self.halve(x)

    def halve(self, x):
        half = x.shape[0] // 2
        high = is_high(*self.order[0])
        self.sent = lax.dynamic_slice_in_dim(x, (1 - high) * half, half)
        self.keep = lax.dynamic_slice_in_dim(x, high * half, half)

    def busy(self):
        return bool(self.order)

    def send(self):
        return self.sent

    def link(self):
        return self.order[0]

    def take(self, got):
        self.got = got
        self.used.append(self.order.pop(0))


class Spread:
    def __init__(self, x, used):
        self.x, self.used = x[None], list(used)

    def busy(self):
        return bool(self.used)

    def send(self):
        return self.x

    def link(self):
        return self.used[-1]

    def take(self, got):
        high = is_high(*self.used.pop())
        pair = jnp.concatenate([got, self.x]), jnp.concatenate([self.x, got])
        self.x = jnp.where(high == 1, *pair)


class Whole:
    def __init__(self, arrays, link):
        self.arrays, self.at = arrays, link
        self.total = None

    def halves(self, high):
        return [
            lax.dynamic_slice_in_dim(x, high * (x.shape[0] // 2), x.shape[0] // 2)
            for x in self.arrays
        ]

    def busy(self):
        return self.total is None

    def send(self):
        return jnp.concatenate(self.halves(1 - is_high(*self.at)))

    def link(self):
        return self.at

    def take(self, got):
        self.total = jnp.concatenate(self.halves(is_high(*self.at))) + got


class Rows:
    def __init__(self, x, sums, joins):
        self.x, self.sums, self.joins = x, list(sums), list(joins)

    def busy(self):
        return bool(self.sums or self.joins)

    def send(self):
        return self.x

    def link(self):
        return self.sums[0] if self.sums else self.joins[0]

    def take(self, got):
        axis, bit = self.link()
        if self.sums:
            self.sums.pop(0)
            self.x = self.x + got
            return
        self.joins.pop(0)
        high = (lax.axis_index(axis) // bit) % 2
        pair = [jnp.concatenate(p, axis=1) for p in ((got, self.x), (self.x, got))]
        self.x = jnp.where(high == 1, *pair)


def beside(flows, first, kernel):
    flows = [flow for flow in flows if flow.busy()]
    first, *sends = lax.optimization_barrier((first, *(flow.send() for flow in flows)))
    got = [swapped(x, *flow.link()) for flow, x in zip(flows, sends)]
    outs = kernel(first)
    head, *got = lax.optimization_barrier((outs[0], *got))
    for flow, x in zip(flows, got):
        flow.take(x)
    folding = [flow for flow in flows if isinstance(flow, Flow)]
    if folding:
        fold(folding)
    return [head] + list(outs[1:])


def swap_two(outs):
    return [outs[1], outs[0]] + list(outs[2:])


def move_first(outs):
    return list(outs[1:]) + [outs[0]]


def messages(message, backward):
    size = lax.axis_size("seq")
    got = []
    for far in range(1, size):
        pairs = [(i, i + far) for i in range(size - far)]
        if backward:
            pairs = [(j, i) for i, j in pairs]
        got.append(lax.ppermute(message, "seq", pairs))
    return got


def body(
    tokens,
    valid_mask,
    timesteps,
    class_ids,
    time_first,
    time_second,
    class_table,
    ada_weight,
    ada_bias,
    conv_taps,
    query_proj,
    key_proj,
    value_proj,
    decay_down,
    decay_up,
    decay_bias,
    gate_proj,
    out_proj,
    mlp_up,
    mlp_down,
    cotangent,
):
    count, length, width = tokens.shape
    size, mine = lax.axis_size("seq"), lax.axis_index("seq")
    tiles, chunks = length // TILE, length // CHUNK
    per_tile = TILE // CHUNK
    up_pairs = [(i, i + 1) for i in range(size - 1)]
    down_pairs = [(j, i) for i, j in up_pairs]
    seq_bits = [("seq", bit) for bit in halves("seq")]
    img_bits = [("img", bit) for bit in halves("img")]
    core, order_a = seq_bits[0], seq_bits[1:] + img_bits
    order_b = img_bits[:2] + seq_bits[1:] + img_bits[2:]

    def borders(x):
        return (
            lax.ppermute(x[:, length - GRID :], "seq", up_pairs),
            lax.ppermute(x[:, :GRID], "seq", down_pairs),
        )

    above, below = borders(tokens)

    square = (width, width)
    row = (length, width)
    dense = 2 * 3 * count * length * width
    each = 4 * count * length * width
    features = time_features(timesteps)
    mod_spec = per_image((6, width))
    modul, info = call(
        condition_kernel,
        (count,),
        [
            per_image((1, FREQ)),
            whole(time_first.shape),
            whole(time_second.shape),
            pl.BlockSpec((8, width), lambda n, ids: (ids[n] // 8, 0)),
            whole(ada_weight.shape),
            whole((6 * width,)),
        ],
        [
            (mod_spec, (count, 6, width)),
            (per_image((8, width)), (count, 8, width)),
        ],
        [],
        flops=1000000,
        moved=4 * 6 * width * width,
        prefetch=1,
    )(class_ids, features[:, None], time_first, time_second, class_table, ada_weight, ada_bias)

    valid = valid_mask[:, None]
    valid_spec = per_image((1, length))
    message_shape = (PAIRS, HEAD_DIM + 8, LANES)
    def tiled(shape=(TILE, width)):
        return pl.BlockSpec((None,) + shape, lambda n, i: (n, i, 0))

    tile_row = (tiled(), (count,) + row)
    pair_spec = pl.BlockSpec(
        (None, per_tile, PAIRS, LANES, LANES), lambda n, i: (n, i, 0, 0, 0)
    )
    state_spec = pl.BlockSpec((None, PAIRS, LANES, LANES), lambda n, i: (n, 0, 0, 0))
    state_shape = (count, PAIRS, LANES, LANES)
    score_shape = (count, chunks, PAIRS, 2 * CHUNK, CHUNK)
    score_spec = pl.BlockSpec(
        (None, per_tile, PAIRS, 2 * CHUNK, CHUNK), lambda n, i: (n, i, 0, 0, 0)
    )
    normed_spec = per_image((length + 2 * GRID, width))
    message_spec = per_image(message_shape)
    fade_spec = pl.BlockSpec((None, per_tile, 8, width), lambda n, i: (n, i, 0, 0))
    (
        weights,
        normed,
        conv,
        query,
        keys,
        values,
        cumul,
        slope,
        far,
        states,
        fades,
        message,
    ) = call(
        front_kernel,
        (count, tiles),
        [
            per_image(row),
            per_image((GRID, width)),
            per_image((GRID, width)),
            valid_spec,
            mod_spec,
            whole((9, width)),
            whole(square),
            whole(square),
            whole(square),
            whole(decay_up.shape),
            whole(decay_up.shape),
            whole((width,)),
        ],
        [
            (whole((width, 4 * width)), (width, 4 * width)),
            (per_image((length + 2 * GRID, width)), (count, length + 2 * GRID, width)),
        ]
        + [tile_row] * 7
        + [
            (pair_spec, (count, chunks, PAIRS, LANES, LANES)),
            (fade_spec, (count, chunks, 8, width)),
            (message_spec, (count,) + message_shape),
        ],
        [
            pltpu.VMEM((6 * width, 4 * width), BF16),
            pltpu.VMEM((TILE, 4 * width), F32),
            pltpu.VMEM((PAIRS, LANES, LANES), F32),
            pltpu.VMEM((8, width), F32),
        ],
        flops=dense * 4 * width,
        moved=each * 10,
    )(
        tokens,
        above,
        below,
        valid,
        modul,
        conv_taps,
        query_proj,
        key_proj,
        value_proj,
        decay_down.T,
        decay_up,
        decay_bias,
    )

    forward_parts = messages(message, False)
    inner, scores, gate_in = call(
        inner_kernel,
        (count, tiles),
        [tiled()] * 4 + [pair_spec, normed_spec, whole(square)],
        [tile_row, (score_spec, score_shape), tile_row],
        [pltpu.VMEM((3 * width, width), BF16), pltpu.VMEM((PAIRS, 2 * CHUNK, CHUNK), F32)],
        flops=dense * 2 * width,
        moved=each * 9,
    )(query, keys, values, cumul, states, normed, gate_proj)

    middle, branch, attended, state_in = call(
        mix_kernel,
        (count, tiles),
        [tiled()] * 4 + [mod_spec, whole(square)] + [message_spec] * (size - 1),
        [tile_row] * 3 + [(state_spec, state_shape)],
        [pltpu.VMEM((3 * width, width), BF16)],
        flops=dense * 2 * width,
        moved=each * 7,
    )(inner, far, tokens, gate_in, modul, out_proj, *forward_parts)

    dmod_spec = per_image((8, width))
    dmod_out = (dmod_spec, (count, 8, width))

    def feed_forward(part, last, *partial):
        return call(
            functools.partial(mlp_kernel, last),
            (count, tiles),
            [
                tiled(),
                tiled(),
                mod_spec,
                pl.BlockSpec((width, BLOCK), lambda n, i: (0, part), pipeline_mode=pl.Buffered(1)),
                pl.BlockSpec((BLOCK, width), lambda n, i: (part, 0), pipeline_mode=pl.Buffered(1)),
            ]
            + [tiled()] * len(partial),
            [tile_row] * 2
            + ([dmod_out] if last else [])
            + [(whole((2 * BLOCK, width)), (2 * BLOCK, width))],
            [
                pltpu.VMEM((3 * width, BLOCK), BF16),
                pltpu.VMEM((2 * width, BLOCK), BF16),
                pltpu.VMEM((2 * BLOCK, width), BF16),
                pltpu.VMEM((BLOCK, 3 * width), BF16),
                pltpu.VMEM((width, BLOCK), F32),
                pltpu.VMEM((width, BLOCK), F32),
            ],
            flops=dense * 6 * BLOCK,
            moved=each * 6,
        )(middle, cotangent, modul, mlp_up, mlp_down, *partial)

    mlp_part, dsec_part, g_mlp_a = feed_forward(0, False)
    block_out, dmid, dmod_mlp, g_mlp_b = feed_forward(1, True, mlp_part, dsec_part)

    datt, dnorm, g_mix, dmod_mix, d_message = call(
        mix_back_kernel,
        (count, tiles),
        [tiled()] * 5
        + [normed_spec, mod_spec, message_spec, whole(square), whole(square)],
        [tile_row] * 2
        + [(whole((2 * width, width)), (2 * width, width)), dmod_out]
        + [(message_spec, (count,) + message_shape)],
        [
            pltpu.VMEM((width, 3 * width), BF16),
            pltpu.VMEM((width, 3 * width), BF16),
            pltpu.VMEM((PAIRS, LANES, LANES), F32),
        ],
        flops=dense * 5 * width,
        moved=each * 8,
    )(dmid, branch, attended, gate_in, far, normed, modul, message, out_proj, gate_proj)
    first = Whole([g_mlp_a, g_mlp_b, g_mix], core)
    (datt,) = beside([first], datt, lambda x: [x])
    cut = 1024
    early = [Flow(first.total[:cut], order_a), Flow(first.total[cut:], order_b)]
    d_message, datt = lax.optimization_barrier((d_message, datt))
    backward_parts = messages(d_message, True)

    dquery, dkeys, dvalues, full = beside(early, datt, lambda x: call(
        inner_back_kernel,
        (count, tiles),
        [tiled()] * 5 + [score_spec, pair_spec, fade_spec, state_spec],
        [tile_row] * 3 + [(pair_spec, (count, chunks, PAIRS, LANES, LANES))],
        [
            pltpu.VMEM((PAIRS, 2 * CHUNK, CHUNK), F32),
            pltpu.VMEM((CHUNK, width), F32),
            pltpu.VMEM((CHUNK, width), F32),
        ],
        flops=dense * 2 * width,
        moved=each * 12,
    )(query, keys, values, cumul, x, scores, states, fades, state_in))

    def turned(shape=(TILE, width)):
        return pl.BlockSpec((None,) + shape, lambda n, i: (n, tiles - 1 - i, 0))

    dconv, dproj, dbias = beside(early, dquery, lambda x: swap_two(call(
        state_back_kernel,
        (count, tiles),
        [valid_spec]
        + [turned()] * 10
        + [
            pl.BlockSpec(
                (None, per_tile, PAIRS, LANES, LANES),
                lambda n, i: (n, tiles - 1 - i, 0, 0, 0),
            ),
            whole((width, 4 * width)),
        ]
        + [message_spec] * (size - 1),
        [
            (turned((TILE, 4 * width)), (count, length, 4 * width)),
            (turned(), (count,) + row),
            (whole((8, width)), (8, width)),
        ],
        [
            pltpu.VMEM((width, 3 * 4 * width), BF16),
            pltpu.VMEM((PAIRS, LANES, LANES), F32),
        ],
        flops=dense * 5 * width,
        moved=each * 16,
    )(
        valid,
        query,
        keys,
        values,
        cumul,
        slope,
        conv,
        datt,
        x,
        dkeys,
        dvalues,
        full,
        weights,
        *backward_parts,
    )))

    d_above, d_below = borders(dconv)
    (g_proj,) = beside(early, dproj, lambda x: call(
        weight_kernel,
        (count, tiles),
        [
            tiled(),
            tiled((TILE, 4 * width)),
            whole((8, width)),
            whole(decay_up.shape),
            whole(decay_up.shape),
        ],
        [(whole((ROWS, width)), (ROWS, width))],
        [pltpu.VMEM((width, 4 * width), F32)],
        flops=dense * 4 * width,
        moved=each * 7,
    )(conv, x, dbias, decay_down.T, decay_up))
    second = Whole([g_proj], core)
    (dconv,) = beside([second], dconv, lambda x: [x])
    late_cut = 384
    late = [Flow(second.total[:late_cut], order_a), Flow(second.total[late_cut:], order_b)]

    dmod_front, dtaps, tokens_grad = beside(early + late, dconv, lambda x: move_first(call(
        front_back_kernel,
        (count, tiles),
        [
            tiled(),
            per_image((length + 2 * GRID, width)),
            per_image(row),
            per_image((GRID, width)),
            per_image((GRID, width)),
            tiled(),
            tiled(),
            mod_spec,
            whole((9, width)),
        ],
        [
            tile_row,
            dmod_out,
            (whole((16, width)), (16, width)),
        ],
        [
            pltpu.VMEM((length + 2 * GRID, width), F32),
            pltpu.VMEM((9, 8, width), F32),
        ],
        flops=count * length * width * 100,
        moved=each * 6,
    )(tokens, normed, x, d_above, d_below, dnorm, dmid, modul, conv_taps)))

    dmod = (dmod_front + dmod_mlp + dmod_mix)[:, :6]
    own = jnp.where(mine == 0, info[:, :3], 0.0)
    ids = jnp.where(mine == 0, class_ids, 0).astype(F32)[:, None, None]
    ids = jnp.broadcast_to(ids, (count, 1, width))
    rows = jnp.moveaxis(jnp.concatenate([dmod, own, ids], axis=1), 1, 0)
    taps = jnp.concatenate([dtaps[:9, None], jnp.zeros((9, count - 1, width), F32)], axis=1)
    flow_r = Rows(jnp.concatenate([rows, taps]), seq_bits, img_bits)
    none = jnp.zeros((), F32)
    while any(flow.busy() for flow in early + late):
        beside([flow_r] + early + late, none, lambda x: [x])
    spread_a, spread_b = (
        Spread(jnp.concatenate([one.keep, two.keep]), one.used) for one, two in zip(early, late)
    )
    while flow_r.busy():
        beside([flow_r, spread_a, spread_b], none, lambda x: [x])
    rows, taps = flow_r.x[:10], jnp.sum(flow_r.x[10:], axis=1)
    images = rows.shape[1]
    ids = rows[9, :, 0].astype(jnp.int32)
    g_first, g_second, g_class, g_ada, g_ada_bias = beside([spread_a, spread_b], rows, lambda x: call(
        embed_kernel,
        (1,),
        [
            whole(rows.shape),
            whole(ada_weight.shape),
            whole(time_second.shape),
        ],
        [
            (whole(shape), shape)
            for shape in (
                time_first.shape,
                time_second.shape,
                class_table.shape,
                ada_weight.shape,
                (1, 6 * width),
            )
        ],
        [],
        flops=images * 2 * 3 * width * width * 14,
        moved=4 * width * width * 20,
        prefetch=1,
    )(ids, x, ada_weight, time_second))
    while spread_a.busy() or spread_b.busy():
        beside([spread_a, spread_b], none, lambda x: [x])
    mine_a, mine_b = spread_a.x, spread_b.x
    other_a, other_b = (swapped(x, *core) for x in (mine_a, mine_b))
    high = is_high(*core)

    def unpacked(x, y):
        rows_a, rows_b = early[0].keep.shape[0], early[1].keep.shape[0]
        flat = [
            part.reshape(-1, width)
            for part in (x[:, :rows_a], y[:, :rows_b], x[:, rows_a:], y[:, rows_b:])
        ]
        return jnp.concatenate(flat[:2]), jnp.concatenate(flat[2:])

    lower = unpacked(jnp.where(high == 0, mine_a, other_a), jnp.where(high == 0, mine_b, other_b))
    upper = unpacked(jnp.where(high == 0, other_a, mine_a), jnp.where(high == 0, other_b, mine_b))

    def pieces(index, start, rows):
        half = rows // 2
        at = slice(start // 2, start // 2 + half)
        return jnp.concatenate([lower[index][at], upper[index][at]])

    mlp_rows = 2 * BLOCK
    g_mlp_a = pieces(0, 0, mlp_rows)
    g_mlp_b = pieces(0, mlp_rows, mlp_rows)
    g_mix = pieces(0, 2 * mlp_rows, 2 * width)
    g_proj = pieces(1, 0, ROWS)

    rank = decay_up.shape[0]
    base = 3 * width
    hidden_rows = 2 * BLOCK

    def joined(first, second):
        return jnp.concatenate(
            [part[j * width : (j + 1) * width] for part in (first, second) for j in range(BLOCK // width)],
            axis=1,
        )

    return (
        block_out,
        tokens_grad,
        g_first,
        g_second,
        g_class,
        g_ada,
        g_ada_bias[0],
        taps,
        g_proj[:width],
        g_proj[width : 2 * width],
        g_proj[2 * width : base],
        g_proj[base : base + rank].T,
        g_proj[base + rank : base + 2 * rank],
        g_proj[base + 2 * rank],
        g_mix[width:],
        g_mix[:width],
        joined(g_mlp_a, g_mlp_b),
        jnp.concatenate([g_mlp_a[BLOCK:], g_mlp_b[BLOCK:hidden_rows]]),
    )


def solution(mesh):
    image, shared = P("img", "seq", None), P()
    return jax.shard_map(
        body,
        mesh=mesh,
        in_specs=(image, P("img", "seq"), P("img"), P("img")) + (shared,) * 16 + (image,),
        out_specs=(image, image) + (shared,) * 16,
        check_vma=False,
    )
```

time: 404 us -> 329 us (0.81)
  blocking collectives: 91 us -> 0 us
  starting transfers between devices: 21.4 us -> 55.7 us
  matrix products: 27.2 us -> 0 us
  waiting for transfers between devices: 45.4 us -> 66.3 us
  between operations: 16.2 us -> 3.13 us
    ppermute x10 -> x43, waiting for transfers between devices: 0.03 us -> 66.3 us  [the longest x33 60.2 us: swapped(): lax.ppermute(x, axis, [(i, i ^ bit) for i in range(lax.axis_size(axis))])]
    psum x2 -> x0, blocking collectives: 47.7 us -> none  [the longest x1 39.2 us: body(): lax.psum((jnp.sum(dtaps, axis=1), g_query, g_key, g_value, g_decay_down,...]
    psum x1 -> x0, waiting for transfers between devices: 45.3 us -> none  [body(): lax.psum((jnp.sum(dtaps, axis=1), g_query, g_key, g_value, g_decay_down,...]
    ppermute x10 -> x43, starting transfers between devices: 21.3 us -> 55.7 us  [the longest x33 34.9 us: swapped(): lax.ppermute(x, axis, [(i, i ^ bit) for i in range(lax.axis_size(axis))])]
    all_gather x1 -> x0, blocking collectives: 30.9 us -> none  [body(): lax.all_gather(jnp.concatenate([lax.psum(dmod, 'seq'), features, first, e...]
    dot_general x13 -> x0, matrix products: 27.2 us -> none  [product(): return jnp.dot(left, right, precision=HIGH, preferred_element_type=F32)]
    unnamed x1 -> x0, blocking collectives: 12.3 us -> none
    unnamed x48 -> x38, local copies, waits for them, and re-layouts: 14.4 us -> 4.55 us
  transfers between devices with their start and end apart: 11 -> 43, of which waited for: 1 -> 16; matrix products, arithmetic and copies ran while one was open for 11% -> 4% of each run, Pallas kernels for 10% -> 22%
where the time goes in v2:
time: 329 us; the launch traced here: 322 us
  Pallas kernels  156 us (47%)
  waiting for transfers between devices  66.3 us (20%)
  starting transfers between devices  55.7 us (17%)
  local copies, waits for them, and re-layouts  23 us (7%)
  other arithmetic  18.6 us (6%)
    ppermute x33, waiting for transfers between devices, swapped(): lax.ppermute(x, axis, [(i, i ^ bit) for i in range(lax.axis_size(axis))])  60.2 us
    pallas_call x2, Pallas kernels, feed_forward(): call(functools.partial(mlp_kernel, last), (count, tiles), [tiled(), tiled...  43.7 us
    ppermute x33, starting transfers between devices, swapped(): lax.ppermute(x, axis, [(i, i ^ bit) for i in range(lax.axis_size(axis))])  34.9 us
    pallas_call x1, Pallas kernels, body(): call(front_kernel, (count, tiles), [per_image(row), per_image((GRID, widt...  19.6 us
    pallas_call x1, Pallas kernels, body(): call(state_back_kernel, (count, tiles), [valid_spec] + [turned()] * 10 +...  15.3 us
    ppermute x6, starting transfers between devices, messages(): got.append(lax.ppermute(message, 'seq', pairs))  13.5 us
    pallas_call x1, Pallas kernels, body(): call(inner_back_kernel, (count, tiles), [tiled()] * 5 + [score_spec, pair...  13 us
    pallas_call x1, Pallas kernels, body(): call(mix_back_kernel, (count, tiles), [tiled()] * 5 + [normed_spec, mod_s...  12.8 us
  transfers between devices with their start and end apart: 43, of which 16 were waited for; matrix products, arithmetic and copies ran while one was open for 4% of the time, Pallas kernels for 22%

profile of v2, /device:TPU:0, one launch (start us, length us, event | category | flops | bytes accessed | tf_op | source)
XLA Modules:
  0.0 322.4 jit_solution(8789813947029265858)
XLA Ops:
  7.2 4.0 %shard_map.340 = (f32[1,6,384]{2,1,0:T(8,128)}, f32[1,8,384]{2,1,0:T(8,128)}) custom-call(s32[1]{0:T(128)S(6)} %copy.48.ids_ref, f32[1,1,256]{2,1,0:T(1,128)} %maximum_bitcast_fusion.3.feat_ref, f32[256,384]{1,0:T(8,128)} %first_w_ref.1, f32[384,384]{1,0:T(8,128)} %second_ref.1, f32[1000,384]{1,0:T(8,128)} %row_ref.1, f32[384,2304]{1,0:T(8,128)} %ada_ref.3, ...), custom_call_target="tpu_custom_call" | custom-call | flops 1 | bytes 1 | tf_op jit(solution)/shard_map/pallas_call | solution.py:1119
  11.9 19.6 %shard_map.341 = (f32[384,1536]{1,0:T(8,128)}, f32[1,1152,384]{2,1,0:T(8,128)}, f32[1,1024,384]{2,1,0:T(8,128)}, f32[1,1024,384]{2,1,0:T(8,128)}, f32[1,1024,384...) custom-call(f32[1,1024,384]{2,1,0:T(8,128)} %tok_ref.5, ...), custom_call_target="tpu_custom_call" | custom-call | flops 1 | bytes 1 | tf_op jit(solution)/shard_map/pallas_call | solution.py:1172
  31.5 4.3 %collective-permute-start.2 = (f32[1,3,72,128]{3,2,1,0:T(8,128)}, f32[1,3,72,128]{3,2,1,0:T(8,128)S(1)}, u32[]{:S(2)}, u32[]{:S(2)}) collective-permute-start(f32[1,3,72,128]{3,2,1,0:T(8,128)} %get-tuple-element.182.message_ref), channel_id=1, source_target_pairs={{0,1},{1,2},{2,3},{4,5},{5,6},{6,7},{8,9},{9,10},{10,11},{12,13},{... | collective-permute-start | bytes 331784 | tf_op jit(solution)/shard_map/ppermute | solution.py:1067
  35.8 3.5 %collective-permute-start.3 = (f32[1,3,72,128]{3,2,1,0:T(8,128)}, f32[1,3,72,128]{3,2,1,0:T(8,128)S(1)}, u32[]{:S(2)}, u32[]{:S(2)}) collective-permute-start(f32[1,3,72,128]{3,2,1,0:T(8,128)} %get-tuple-element.182.message_ref), channel_id=1, source_target_pairs={{0,2},{1,3},{4,6},{5,7},{8,10},{9,11},{12,14},{13,15},{16,18},{17,... | collective-permute-start | bytes 331784 | tf_op jit(solution)/shard_map/ppermute | solution.py:1067
  40.9 11.5 %shard_map.342 = (f32[1,1024,384]{2,1,0:T(8,128)}, f32[1,8,3,256,128]{4,3,2,1,0:T(8,128)}, f32[1,1024,384]{2,1,0:T(8,128)}) custom-call(f32[1,1024,384]{2,1,0:T(8,128)} %get-tuple-element.173.q_ref, f32[1,1024,384]{2,1,0:T(8,128)} %get-tuple-element.174.k_ref, f32[1,1024,384]{2,1,0:T(8,128)} %get-tuple-element.175.v_ref, ...), custom_call_target="tpu_custom_call" | custom-call | flops 1 | bytes 1 | tf_op jit(solution)/shard_map/pallas_call | solution.py:1223
  53.1 7.8 %shard_map.343 = (f32[1,1024,384]{2,1,0:T(8,128)}, f32[1,1024,384]{2,1,0:T(8,128)}, f32[1,1024,384]{2,1,0:T(8,128)}, f32[1,3,128,128]{3,2,1,0:T(8,128)}) custom-call(f32[1,1024,384]{2,1,0:T(8,128)} %get-tuple-element.179.o_ref, f32[1,1024,384]{2,1,0:T(8,128)} %get-tuple-element.180.far_ref, f32[1,1024,384]{2,1,0:T(8,128)} %tok_ref.5, ...), custom_call_target="tpu_custom_call" | custom-call | flops 1 | bytes 1 | tf_op jit(solution)/shard_map/pallas_call | solution.py:1233
  60.8 21.3 %shard_map.344 = (f32[1,1024,384]{2,1,0:T(8,128)}, f32[1,1024,384]{2,1,0:T(8,128)}, f32[1536,384]{1,0:T(8,128)}) custom-call(f32[1,1024,384]{2,1,0:T(8,128)} %get-tuple-element.183.mid_ref, f32[1,1024,384]{2,1,0:T(8,128)} %cot_ref.3, f32[1,6,384]{2,1,0:T(8,128)} %get-tuple-element.172.mod_ref, f32[384,1536]{1,0:T(8,128)} %up_ref.6, f32[1536,384]{1,0:T(8,128)} %down_ref.3), custom_call_target="tpu_custom_call" | custom-call | flops 1 | bytes 1 | tf_op jit(solution)/shard_map/pallas_call | solution.py:1247
  82.1 22.4 %shard_map.345 = (f32[1,1024,384]{2,1,0:T(8,128)}, f32[1,1024,384]{2,1,0:T(8,128)}, f32[1,8,384]{2,1,0:T(8,128)}, f32[1536,384]{1,0:T(8,128)}) custom-call(f32[1,1024,384]{2,1,0:T(8,128)} %get-tuple-element.183.mid_ref, f32[1,1024,384]{2,1,0:T(8,128)} %cot_ref.3, f32[1,6,384]{2,1,0:T(8,128)} %get-tuple-element.172.mod_ref, f32[384,1536]{1,0:T(8,128)} %up_ref.6, ...), custom_call_target="tpu_custom_call" | custom-call | flops 1 | bytes 1 | tf_op jit(solution)/shard_map/pallas_call | solution.py:1247
  108.1 12.8 %shard_map.346 = (f32[1,1024,384]{2,1,0:T(8,128)}, f32[1,1024,384]{2,1,0:T(8,128)}, f32[768,384]{1,0:T(8,128)}, f32[1,8,384]{2,1,0:T(8,128)}, f32[1,3,72,128]{3,2,1,0:T(8,128)}) custom-call(f32[1,1024,384]{2,1,0:T(8,128)} %get-tuple-element.189.dmid_ref, f32[1,1024,384]{2,1,0:T(8,128)} %get-tuple-element.190.branch_ref, ...), custom_call_target="tpu_custom_call" | custom-call | flops 1 | bytes 1 | tf_op jit(solution)/shard_map/pallas_call | solution.py:1276
  124.9 5.7 %collective-permute-done.5 = f32[1920,384]{1,0:T(8,128)} collective-permute-done((f32[1920,384]{1,0:T(8,128)}, f32[1920,384]{1,0:T(8,128)}, u32[]{:S(2)}, u32[]{:S(2)}) %collective-permute-start.5) | collective-permute-done | bytes 2949152 | tf_op jit(solution)/shard_map/ppermute | solution.py:893
  137.8 13.0 %shard_map.347 = (f32[1,1024,384]{2,1,0:T(8,128)}, f32[1,1024,384]{2,1,0:T(8,128)}, f32[1,1024,384]{2,1,0:T(8,128)}, f32[1,8,3,128,128]{4,3,2,1,0:T(8,128)}) custom-call(f32[1,1024,384]{2,1,0:T(8,128)} %get-tuple-element.173.q_ref, f32[1,1024,384]{2,1,0:T(8,128)} %get-tuple-element.174.k_ref, f32[1,1024,384]{2,1,0:T(8,128)} %get-tuple-element.175.v_ref, ...), custom_call_target="tpu_custom_call" | custom-call | flops 1 | bytes 1 | tf_op jit(solution)/shard_map/pallas_call | solution.py:1299
  150.9 3.1 collective-permute-done.7.refs_3_
  166.7 3.4 %collective-permute-done.9.rest_1_ = f32[1,3,72,128]{3,2,1,0:T(8,128)S(1)} collective-permute-done((f32[1,3,72,128]{3,2,1,0:T(8,128)S(1)}, f32[1,3,72,128]{3,2,1,0:T(8,128)S(1)}, u32[]{:S(2)}, u32[]{:S(2)}) %collective-permute-start.9) | collective-permute-done | bytes 110624 | tf_op jit(solution)/shard_map/ppermute | solution.py:1067
  170.7 15.3 %shard_map.349 = (f32[1,1024,1536]{2,1,0:T(8,128)}, f32[1,1024,384]{2,1,0:T(8,128)}, f32[8,384]{1,0:T(8,128)}) custom-call(s32[1,1,1024]{2,1,0:T(1,128)} %bitcast.49, f32[1,1024,384]{2,1,0:T(8,128)} %get-tuple-element.173.q_ref, f32[1,1024,384]{2,1,0:T(8,128)} %get-tuple-element.174.k_ref, f32[1,1024,384]{2,1,0:T(8,128)} %get-tuple-element.175.v_ref, ...), custom_call_target="tpu_custom_call" | custom-call | flops 1 | bytes 1 | tf_op jit(solution)/shard_map/pallas_call | solution.py:1316
  186.7 10.0 %shard_map.351 = f32[1280,384]{1,0:T(8,128)} custom-call(f32[1,1024,384]{2,1,0:T(8,128)} %get-tuple-element.188.conv_ref, f32[1,1024,1536]{2,1,0:T(8,128)} %get-tuple-element.231.proj_ref, f32[8,384]{1,0:T(8,128)} %get-tuple-element.232.dbias_ref, f32[16,384]{1,0:T(8,128)} %bitcast.46, f32[16,384]{1,0:T(8,128)} %up_ref.7), custom_call_target="tpu_custom_call" | custom-call | flops 1 | bytes 1 | tf_op jit(solution)/shard_map/pallas_call | solution.py:1358
  211.8 7.8 %shard_map.353 = (f32[1,1024,384]{2,1,0:T(8,128)}, f32[1,8,384]{2,1,0:T(8,128)}, f32[16,384]{1,0:T(8,128)}) custom-call(f32[1,1024,384]{2,1,0:T(8,128)} %tok_ref.5, f32[1,1152,384]{2,1,0:T(8,128)} %get-tuple-element.178.normed_ref, f32[1,1024,384]{2,1,0:T(8,128)} %get-tuple-element.246.dconv_ref, f32[1,64,384]{2,1,0:T(8,128)} %copy-done.10, ...), custom_call_target="tpu_custom_call" | custom-call | flops 1 | bytes 1 | tf_op jit(solution)/shard_map/pallas_call | solution.py:1378
  231.8 3.8 %collective-permute-done.25 = f32[19,1,384]{2,1,0:T(1,128)S(1)} collective-permute-done((f32[19,1,384]{2,1,0:T(1,128)S(1)}, f32[19,1,384]{2,1,0:T(1,128)S(1)}, u32[]{:S(2)}, u32[]{:S(2)}) %collective-permute-start.25) | collective-permute-done | bytes 29216 | tf_op jit(solution)/shard_map/ppermute | solution.py:893
  240.2 4.6 %collective-permute-done.30.refs_3_ = f32[16,384]{1,0:T(8,128)S(1)} collective-permute-done((f32[16,384]{1,0:T(8,128)S(1)}, f32[16,384]{1,0:T(8,128)S(1)}, u32[]{:S(2)}, u32[]{:S(2)}) %collective-permute-start.30) | collective-permute-done | bytes 24608 | tf_op jit(solution)/shard_map/ppermute | solution.py:893
  245.2 2.8 collective-permute-start.33
  248.3 7.8 %collective-permute-done.31 = f32[19,2,384]{2,1,0:T(2,128)S(1)} collective-permute-done((f32[19,2,384]{2,1,0:T(2,128)S(1)}, f32[19,2,384]{2,1,0:T(2,128)S(1)}, u32[]{:S(2)}, u32[]{:S(2)}) %collective-permute-start.31) | collective-permute-done | bytes 58400 | tf_op jit(solution)/shard_map/ppermute | solution.py:893
  258.4 5.2 %collective-permute-done.34 = f32[19,4,384]{2,1,0:T(4,128)S(1)} collective-permute-done((f32[19,4,384]{2,1,0:T(4,128)S(1)}, f32[19,4,384]{2,1,0:T(4,128)S(1)}, u32[]{:S(2)}, u32[]{:S(2)}) %collective-permute-start.34) | collective-permute-done | bytes 116768 | tf_op jit(solution)/shard_map/ppermute | solution.py:893
  268.0 9.0 %shard_map.358 = (f32[256,384]{1,0:T(8,128)}, f32[384,384]{1,0:T(8,128)}, f32[1000,384]{1,0:T(8,128)}, f32[384,2304]{1,0:T(8,128)}, f32[1,2304]{1,0:T(1,128)}) custom-call(s32[8]{0:T(128)} %fusion.3.ids_ref, f32[10,8,384]{2,1,0:T(8,128)} %slice.183.rows_ref, f32[384,2304]{1,0:T(8,128)} %ada_ref.3, f32[384,384]{1,0:T(8,128)} %second_ref.1), custom_call_target="tpu_custom_call" | custom-call | flops 1 | bytes 1 | tf_op jit(solution)/shard_map/pallas_call | solution.py:1423
  282.7 17.6 %collective-permute-done.40 = f32[8,72,384]{2,1,0:T(8,128)S(1)} collective-permute-done((f32[8,72,384]{2,1,0:T(8,128)S(1)}, f32[8,72,384]{2,1,0:T(8,128)S(1)}, u32[]{:S(2)}, u32[]{:S(2)}) %collective-permute-start.40) | collective-permute-done | bytes 884768 | tf_op jit(solution)/shard_map/ppermute | solution.py:893
  300.3 2.8 collective-permute-done.39
  (187 shorter events, 100.1 us)
Async XLA Ops:
  1.6 9.6 %collective-permute-start = (f32[1,64,384]{2,1,0:T(8,128)S(1)}, f32[1,64,384]{2,1,0:T(8,128)S(1)}, u32[]{:S(2)}, u32[]{:S(2)}) collective-permute-start(f32[1,64,384]{2,1,0:T(8,128)S(1)} %get-tuple-element.343), channel_id=1, source_target_pairs={{0,1},{1,2},{2,3},{4,5},{5,6},{6,7},{8,9},{9,10},{10,11},{12,13},{... | collective-permute-start | bytes 294920 | tf_op jit(solution)/shard_map/ppermute | solution.py:1107
  31.5 20.9 %collective-permute-start.2 = (f32[1,3,72,128]{3,2,1,0:T(8,128)}, f32[1,3,72,128]{3,2,1,0:T(8,128)S(1)}, u32[]{:S(2)}, u32[]{:S(2)}) collective-permute-start(f32[1,3,72,128]{3,2,1,0:T(8,128)} %get-tuple-element.182.message_ref), channel_id=1, source_target_pairs={{0,1},{1,2},{2,3},{4,5},{5,6},{6,7},{8,9},{9,10},{10,11},{12,13},{... | collective-permute-start | bytes 331784 | tf_op jit(solution)/shard_map/ppermute | solution.py:1067
  35.8 16.5 %collective-permute-start.3 = (f32[1,3,72,128]{3,2,1,0:T(8,128)}, f32[1,3,72,128]{3,2,1,0:T(8,128)S(1)}, u32[]{:S(2)}, u32[]{:S(2)}) collective-permute-start(f32[1,3,72,128]{3,2,1,0:T(8,128)} %get-tuple-element.182.message_ref), channel_id=1, source_target_pairs={{0,2},{1,3},{4,6},{5,7},{8,10},{9,11},{12,14},{13,15},{16,18},{17,... | collective-permute-start | bytes 331784 | tf_op jit(solution)/shard_map/ppermute | solution.py:1067
  39.4 13.0 %collective-permute-start.4 = (f32[1,3,72,128]{3,2,1,0:T(8,128)}, f32[1,3,72,128]{3,2,1,0:T(8,128)S(1)}, u32[]{:S(2)}, u32[]{:S(2)}) collective-permute-start(f32[1,3,72,128]{3,2,1,0:T(8,128)} %get-tuple-element.182.message_ref), channel_id=1, source_target_pairs={{0,3},{4,7},{8,11},{12,15},{16,19},{20,23},{24,27},{28,31}} | collective-permute-start | bytes 331784 | tf_op jit(solution)/shard_map/ppermute | solution.py:1067
  136.2 19.6 %collective-permute-start.6 = (f32[512,384]{1,0:T(8,128)S(1)}, f32[512,384]{1,0:T(8,128)S(1)}, u32[]{:S(2)}, u32[]{:S(2)}) collective-permute-start(f32[512,384]{1,0:T(8,128)S(1)} %get-tuple-element.207), channel_id=1, source_target_pairs={{0,2},{1,3},{2,0},{3,1},{4,6},{5,7},{6,4},{7,5},{8,10},{9,11},{10,... | collective-permute-start | bytes 2359304 | tf_op jit(solution)/shard_map/ppermute | solution.py:893
  136.3 17.8 %collective-permute-start.7 = (f32[448,384]{1,0:T(8,128)}, f32[448,384]{1,0:T(8,128)S(1)}, u32[]{:S(2)}, u32[]{:S(2)}) collective-permute-start(f32[448,384]{1,0:T(8,128)} %get-tuple-element.208), channel_id=1, source_target_pairs={{0,4},{4,0},{8,12},{12,8},{16,20},{20,16},{24,28},{28,24},{1,5},{5... | collective-permute-start | bytes 2064392 | tf_op jit(solution)/shard_map/ppermute | solution.py:893
  156.7 29.3 %collective-permute-start.11 = (f32[256,384]{1,0:T(8,128)S(1)}, f32[256,384]{1,0:T(8,128)S(1)}, u32[]{:S(2)}, u32[]{:S(2)}) collective-permute-start(f32[256,384]{1,0:T(8,128)S(1)} %get-tuple-element.221), channel_id=1, source_target_pairs={{0,4},{4,0},{8,12},{12,8},{16,20},{20,16},{24,28},{28,24},{1,5},{5... | collective-permute-start | bytes 1179656 | tf_op jit(solution)/shard_map/ppermute | solution.py:893
  158.2 27.8 %collective-permute-start.12 = (f32[224,384]{1,0:T(8,128)}, f32[224,384]{1,0:T(8,128)S(1)}, u32[]{:S(2)}, u32[]{:S(2)}) collective-permute-start(f32[224,384]{1,0:T(8,128)} %get-tuple-element.222), channel_id=1, source_target_pairs={{0,8},{4,12},{8,0},{12,4},{16,24},{20,28},{24,16},{28,20},{1,9},{5... | collective-permute-start | bytes 1032200 | tf_op jit(solution)/shard_map/ppermute | solution.py:893
  186.1 10.5 %collective-permute-start.13 = (f32[128,384]{1,0:T(8,128)S(1)}, f32[128,384]{1,0:T(8,128)S(1)}, u32[]{:S(2)}, u32[]{:S(2)}) collective-permute-start(f32[128,384]{1,0:T(8,128)S(1)} %get-tuple-element.233), channel_id=1, source_target_pairs={{0,8},{4,12},{8,0},{12,4},{16,24},{20,28},{24,16},{28,20},{1,9},{5... | collective-permute-start | bytes 589832 | tf_op jit(solution)/shard_map/ppermute | solution.py:893
  186.7 10.0 %collective-permute-start.14 = (f32[112,384]{1,0:T(8,128)S(1)}, f32[112,384]{1,0:T(8,128)S(1)}, u32[]{:S(2)}, u32[]{:S(2)}) collective-permute-start(f32[112,384]{1,0:T(8,128)S(1)} %get-tuple-element.234), channel_id=1, source_target_pairs={{0,2},{1,3},{2,0},{3,1},{4,6},{5,7},{6,4},{7,5},{8,10},{9,11},{10,... | collective-permute-start | bytes 516104 | tf_op jit(solution)/shard_map/ppermute | solution.py:893
  200.0 10.7 %collective-permute-start.16 = (f32[1,64,384]{2,1,0:T(8,128)S(1)}, f32[1,64,384]{2,1,0:T(8,128)S(1)}, u32[]{:S(2)}, u32[]{:S(2)}) collective-permute-start(f32[1,64,384]{2,1,0:T(8,128)S(1)} %get-tuple-element.339), channel_id=1, source_target_pairs={{0,1},{1,2},{2,3},{4,5},{5,6},{6,7},{8,9},{9,10},{10,11},{12,13},{... | collective-permute-start | bytes 294920 | tf_op jit(solution)/shard_map/ppermute | solution.py:1107
  204.1 16.3 %collective-permute-start.20 = (f32[192,384]{1,0:T(8,128)S(1)}, f32[192,384]{1,0:T(8,128)S(1)}, u32[]{:S(2)}, u32[]{:S(2)}) collective-permute-start(f32[192,384]{1,0:T(8,128)S(1)} %get-tuple-element.252), channel_id=1, source_target_pairs={{0,2},{1,3},{2,0},{3,1},{4,6},{5,7},{6,4},{7,5},{8,10},{9,11},{10,... | collective-permute-start | bytes 884744 | tf_op jit(solution)/shard_map/ppermute | solution.py:893
  207.5 12.9 %collective-permute-start.21 = (f32[128,384]{1,0:T(8,128)S(1)}, f32[128,384]{1,0:T(8,128)S(1)}, u32[]{:S(2)}, u32[]{:S(2)}) collective-permute-start(f32[128,384]{1,0:T(8,128)S(1)} %get-tuple-element.253), channel_id=1, source_target_pairs={{0,4},{4,0},{8,12},{12,8},{16,20},{20,16},{24,28},{28,24},{1,5},{5... | collective-permute-start | bytes 589832 | tf_op jit(solution)/shard_map/ppermute | solution.py:893
  208.0 12.3 %collective-permute-start.18 = (f32[64,384]{1,0:T(8,128)S(1)}, f32[64,384]{1,0:T(8,128)S(1)}, u32[]{:S(2)}, u32[]{:S(2)}) collective-permute-start(f32[64,384]{1,0:T(8,128)S(1)} %get-tuple-element.250), channel_id=1, source_target_pairs={{0,16},{4,20},{8,24},{12,28},{16,0},{20,4},{24,8},{28,12},{1,17},{... | collective-permute-start | bytes 294920 | tf_op jit(solution)/shard_map/ppermute | solution.py:893
  210.6 9.7 %collective-permute-start.19 = (f32[56,384]{1,0:T(8,128)S(1)}, f32[56,384]{1,0:T(8,128)S(1)}, u32[]{:S(2)}, u32[]{:S(2)}) collective-permute-start(f32[56,384]{1,0:T(8,128)S(1)} %get-tuple-element.251), channel_id=1, source_target_pairs={{0,16},{4,20},{8,24},{12,28},{16,0},{20,4},{24,8},{28,12},{1,17},{... | collective-permute-start | bytes 258056 | tf_op jit(solution)/shard_map/ppermute | solution.py:893
  235.8 9.0 %collective-permute-start.29 = (f32[24,384]{1,0:T(8,128)S(1)}, f32[24,384]{1,0:T(8,128)S(1)}, u32[]{:S(2)}, u32[]{:S(2)}) collective-permute-start(f32[24,384]{1,0:T(8,128)S(1)} %get-tuple-element.288), channel_id=1, source_target_pairs={{0,16},{4,20},{8,24},{12,28},{16,0},{20,4},{24,8},{28,12},{1,17},{... | collective-permute-start | bytes 110600 | tf_op jit(solution)/shard_map/ppermute | solution.py:893
  245.0 11.1 %collective-permute-start.32 = (f32[1,88,384]{2,1,0:T(8,128)S(1)}, f32[1,88,384]{2,1,0:T(8,128)S(1)}, u32[]{:S(2)}, u32[]{:S(2)}) collective-permute-start(f32[1,88,384]{2,1,0:T(8,128)S(1)} %maximum_bitcast_fusion), channel_id=1, source_target_pairs={{0,16},{4,20},{8,24},{12,28},{16,0},{20,4},{24,8},{28,12},{1,17},{... | collective-permute-start | bytes 405512 | tf_op jit(solution)/shard_map/ppermute | solution.py:893
  245.2 10.9 %collective-permute-start.33 = (f32[1,72,384]{2,1,0:T(8,128)S(1)}, f32[1,72,384]{2,1,0:T(8,128)S(1)}, u32[]{:S(2)}, u32[]{:S(2)}) collective-permute-start(f32[1,72,384]{2,1,0:T(8,128)S(1)} %maximum_bitcast_fusion.1), channel_id=1, source_target_pairs={{0,16},{4,20},{8,24},{12,28},{16,0},{20,4},{24,8},{28,12},{1,17},{... | collective-permute-start | bytes 331784 | tf_op jit(solution)/shard_map/ppermute | solution.py:893
  256.2 9.6 %collective-permute-start.35 = (f32[2,88,384]{2,1,0:T(8,128)S(1)}, f32[2,88,384]{2,1,0:T(8,128)S(1)}, u32[]{:S(2)}, u32[]{:S(2)}) collective-permute-start(f32[2,88,384]{2,1,0:T(8,128)S(1)} %maximum_select_fusion.6), channel_id=1, source_target_pairs={{0,8},{4,12},{8,0},{12,4},{16,24},{20,28},{24,16},{28,20},{1,9},{5... | collective-permute-start | bytes 811016 | tf_op jit(solution)/shard_map/ppermute | solution.py:893
  266.6 12.6 %collective-permute-start.37 = (f32[4,88,384]{2,1,0:T(8,128)S(1)}, f32[4,88,384]{2,1,0:T(8,128)S(1)}, u32[]{:S(2)}, u32[]{:S(2)}) collective-permute-start(f32[4,88,384]{2,1,0:T(8,128)S(1)} %maximum_select_fusion.4), channel_id=1, source_target_pairs={{0,4},{4,0},{8,12},{12,8},{16,20},{20,16},{24,28},{28,24},{1,5},{5... | collective-permute-start | bytes 1622024 | tf_op jit(solution)/shard_map/ppermute | solution.py:893
  267.4 9.9 %collective-permute-start.38 = (f32[4,72,384]{2,1,0:T(8,128)S(1)}, f32[4,72,384]{2,1,0:T(8,128)S(1)}, u32[]{:S(2)}, u32[]{:S(2)}) collective-permute-start(f32[4,72,384]{2,1,0:T(8,128)S(1)} %maximum_select_fusion.5), channel_id=1, source_target_pairs={{0,8},{4,12},{8,0},{12,4},{16,24},{20,28},{24,16},{28,20},{1,9},{5... | collective-permute-start | bytes 1327112 | tf_op jit(solution)/shard_map/ppermute | solution.py:893
  279.4 23.6 %collective-permute-start.39 = (f32[8,88,384]{2,1,0:T(8,128)S(1)}, f32[8,88,384]{2,1,0:T(8,128)S(1)}, u32[]{:S(2)}, u32[]{:S(2)}) collective-permute-start(f32[8,88,384]{2,1,0:T(8,128)S(1)} %maximum_select_fusion.2), channel_id=1, source_target_pairs={{0,2},{1,3},{2,0},{3,1},{4,6},{5,7},{6,4},{7,5},{8,10},{9,11},{10,... | collective-permute-start | bytes 3244040 | tf_op jit(solution)/shard_map/ppermute | solution.py:893
  280.9 19.3 %collective-permute-start.40 = (f32[8,72,384]{2,1,0:T(8,128)S(1)}, f32[8,72,384]{2,1,0:T(8,128)S(1)}, u32[]{:S(2)}, u32[]{:S(2)}) collective-permute-start(f32[8,72,384]{2,1,0:T(8,128)S(1)} %maximum_select_fusion.3), channel_id=1, source_target_pairs={{0,4},{4,0},{8,12},{12,8},{16,20},{20,16},{24,28},{28,24},{1,5},{5... | collective-permute-start | bytes 2654216 | tf_op jit(solution)/shard_map/ppermute | solution.py:893
  304.5 9.7 %collective-permute-start.41 = (f32[16,88,384]{2,1,0:T(8,128)S(1)}, f32[16,88,384]{2,1,0:T(8,128)}, u32[]{:S(2)}, u32[]{:S(2)}) collective-permute-start(f32[16,88,384]{2,1,0:T(8,128)S(1)} %maximum_select_fusion), channel_id=1, source_target_pairs={{0,1},{1,0},{2,3},{3,2},{4,5},{5,4},{6,7},{7,6},{8,9},{9,8},{10,11... | collective-permute-start | bytes 6488072 | tf_op jit(solution)/shard_map/ppermute | solution.py:893
  (39 other events, 164.0 us)
